TPU v7x, 256 devices: a whole 4x4x8 slice. The times are simulated.
256 devices in a mesh: dom: 16 (over z, core), grp: 16 (over y, x).
Axes of the slice: x: 4, y: 4, z: 8, core: 2. Of those that a mesh axis runs over, the one named last changes fastest.
Arguments:
- node_latent: bfloat16 [262144, 128], P(('dom', 'grp')), may hold values from -6 to 6
- node_tangent: bfloat16 [262144, 128], P(('dom', 'grp')), may hold values from -6 to 6
- edge_latent: bfloat16 [1048576, 128], P(('dom', 'grp')), may hold values from -6 to 6
- node_counts: int32 [256], P(('dom', 'grp')), may hold values from 512 to 1024, as said below
- edge_counts: int32 [256], P(('dom', 'grp')), may hold values from 2048 to 4096, as said below
- send_lists: int32 [256, 4, 128], P(('dom', 'grp')), may hold values from 0 to 1023, as said below
- edge_source: int32 [256, 4096], P(('dom', 'grp')), may hold values from 0 to 1535, as said below
- edge_target: int32 [256, 4096], P(('dom', 'grp')), may hold values from 0 to 1023, as said below
- coarse_owner: int32 [256, 1024], P(('dom', 'grp')), may hold values from 0 to 511
- coarse_source: int32 [8192, 8], P(('dom', 'grp')), may hold values from 0 to 1535, as said below
- edge_first: bfloat16 [384, 128], replicated, may hold values from -0.3125 to 0.3125
- edge_second: bfloat16 [128, 128], replicated, may hold values from -0.5 to 0.5
- node_first: bfloat16 [256, 128], replicated, may hold values from -0.375 to 0.375
- node_second: bfloat16 [128, 128], replicated, may hold values from -0.5 to 0.5
- message_first: bfloat16 [256, 128], replicated, may hold values from -0.375 to 0.375
- message_second: bfloat16 [128, 128], replicated, may hold values from -0.5 to 0.5
- coarse_first: bfloat16 [256, 128], replicated, may hold values from -0.375 to 0.375
- coarse_second: bfloat16 [128, 128], replicated, may hold values from -0.5 to 0.5
- prolong_first: bfloat16 [256, 128], replicated, may hold values from -0.375 to 0.375
- prolong_second: bfloat16 [128, 128], replicated, may hold values from -0.5 to 0.5
Outputs:
- node_output: bfloat16 [262144, 128], P(('dom', 'grp'))
- tangent_output: bfloat16 [262144, 128], P(('dom', 'grp'))
Inputs may be any that keep to these rules, and one draw needn't show every extreme that they name: node_counts[p] is at least half of 1024; some partition has all 1024 slots valid. edge_counts[p] is at least half of 4096; some partition has all 4096 slots valid. `send_lists`: every entry is a valid node row of its own partition (below node_counts[p]). `edge_source`: every entry is either a valid node row of the partition (below node_counts[p]) or a halo row 1024 + r with r < 512. `edge_target`: every entry is a valid node row of the partition. `coarse_source`: entries below 32 * 16 name nodes of row d-1, entries from 2 * 32 * 16 on name nodes of row d+1, the others nodes of row d itself.
All inputs are finite; a program needn't handle non-finite values.
Results may differ from a plain program's by a relative error of at most 0.012.
Values may be sent and summed in bfloat16 or wider, within the bound.
A program may use at most 64 MiB of HBM per device.

v0:
```python
import math

import jax
import jax.numpy as jnp
from jax import lax
from jax.sharding import PartitionSpec as P


def from_behind(x, axis, by):
    size = lax.axis_size(axis)
    pairs = [(i, i + by) for i in range(size) if 0 <= i + by < size]
    return lax.ppermute(x, axis, pairs)


def in_blocks(x, dim, size):
    dims = x.shape
    pieces = x.reshape(*dims[:dim], size, dims[dim] // size, *dims[dim + 1 :])
    return jnp.moveaxis(pieces, dim, 0)


def sum_at_owner(x, axis, dim):
    pieces = in_blocks(x, dim, lax.axis_size(axis))
    arrived = lax.all_to_all(pieces, axis, split_axis=0, concat_axis=0, tiled=True)
    return arrived.astype(jnp.float32).sum(axis=0)


def in_order(pieces, dim):
    pieces = jnp.moveaxis(pieces, 0, dim)
    dims = pieces.shape
    return pieces.reshape(*dims[:dim], dims[dim] * dims[dim + 1], *dims[dim + 2 :])


def sent_to_all(x, axis):
    copies = jnp.broadcast_to(x, (lax.axis_size(axis), *x.shape))
    return lax.all_to_all(copies, axis, split_axis=0, concat_axis=0, tiled=True)


def gathered_copies(x, axis, dim):
    return in_order(sent_to_all(x, axis), dim)


def extended(x, sides, width):
    for axis, dim in sides:
        size, length = (lax.axis_size(axis), x.shape[dim])
        up = [(i, (i + 1) % size) for i in range(size - 1)]
        down = [(j, i) for i, j in up]
        last = lax.slice_in_dim(x, length - width, length, axis=dim)
        first = lax.slice_in_dim(x, 0, width, axis=dim)
        before = lax.ppermute(last, axis, up)
        after = lax.ppermute(first, axis, down)
        x = jnp.concatenate([before, x, after], axis=dim)
    return x


def layer_norm(value):
    centred = value - jnp.mean(value, axis=-1, keepdims=True)
    spread = jnp.mean(centred * centred, axis=-1, keepdims=True)
    return centred * lax.rsqrt(spread + 1e-05)


def perceptron(inputs, first, second):
    hidden = jax.nn.silu(jnp.dot(inputs, first, preferred_element_type=jnp.float32)).astype(
        jnp.bfloat16
    )
    return jnp.dot(hidden, second, preferred_element_type=jnp.float32)


def edge_update(edges, source, target, first, second):
    joined = jnp.concatenate([edges, source, target], axis=-1)
    return (edges.astype(jnp.float32) + layer_norm(perceptron(joined, first, second))).astype(
        jnp.bfloat16
    )


def node_update(nodes, other, first, second):
    joined = jnp.concatenate([nodes, other], axis=-1)
    return (nodes.astype(jnp.float32) + layer_norm(perceptron(joined, first, second))).astype(
        jnp.bfloat16
    )


def coarse_update(table, sources, mine, weights):
    message_first, message_second, coarse_first, coarse_second = weights
    senders = table[sources]
    receivers = jnp.broadcast_to(mine[:, None, :], senders.shape)
    joined = jnp.concatenate([senders, receivers], axis=-1).reshape(-1, 2 * senders.shape[-1])
    terms = perceptron(joined, message_first, message_second).reshape(senders.shape)
    message = jnp.sum(terms, axis=1).astype(jnp.bfloat16)
    joined = jnp.concatenate([mine, message], axis=-1)
    return layer_norm(perceptron(joined, coarse_first, coarse_second)).astype(jnp.bfloat16)


def select_rows(indices, count, values):
    selector = (indices[:, None] == jnp.arange(count)[None, :]).astype(jnp.bfloat16)
    return jnp.dot(selector, values, preferred_element_type=jnp.float32).astype(jnp.bfloat16)


def per_device(
    node_latent,
    node_tangent,
    edge_latent,
    node_counts,
    edge_counts,
    send_lists,
    edge_source,
    edge_target,
    coarse_owner,
    coarse_source,
    edge_first,
    edge_second,
    node_first,
    node_second,
    message_first,
    message_second,
    coarse_first,
    coarse_second,
    prolong_first,
    prolong_second,
):
    width = node_latent.shape[1]
    slots = node_latent.shape[0]
    paired = jnp.concatenate([node_latent, node_tangent], axis=1)
    rim_rows = send_lists.shape[2]
    sent = select_rows(send_lists[0].reshape(-1), slots, paired).reshape(4, rim_rows, 2 * width)
    received = []
    for block, offset in ((0, 1), (1, -1)):
        received.append(from_behind(sent[block], "dom", offset))
    for block, offset in ((2, 1), (3, -1)):
        received.append(from_behind(sent[block], "grp", offset))
    table = jnp.concatenate([paired] + received, axis=0)
    table_rows = table.shape[0]
    edge_slots = edge_latent.shape[0]
    block_rows = math.gcd(edge_slots, 512)
    block_count = edge_slots // block_rows
    edge_blocks = edge_latent.reshape(block_count, block_rows, width)
    source_blocks = edge_source[0].reshape(block_count, block_rows)
    target_blocks = edge_target[0].reshape(block_count, block_rows)
    edge_total = edge_counts[0]

    def edge_block(carry, items):
        edges, source, target, number = items
        sender = select_rows(source, table_rows, table)
        target_pick = (target[:, None] == jnp.arange(slots)[None, :]).astype(jnp.bfloat16)
        receiver = jnp.dot(target_pick, paired, preferred_element_type=jnp.float32).astype(
            jnp.bfloat16
        )
        edge_new, edge_tan = jax.jvp(
            lambda a, b, c: edge_update(a, b, c, edge_first, edge_second),
            (edges, sender[:, :width], receiver[:, :width]),
            (jnp.zeros_like(edges), sender[:, width:], receiver[:, width:]),
        )
        live = (number * block_rows + jnp.arange(block_rows) < edge_total)[:, None]
        pair = jnp.concatenate([edge_new, edge_tan], axis=1)
        pair = jnp.where(live, pair, jnp.zeros_like(pair))
        added = jnp.einsum("es,ef->sf", target_pick, pair, preferred_element_type=jnp.float32)
        return (carry + added, None)

    start_sum = jnp.zeros((slots, 2 * width), jnp.float32)
    agg_pair, _ = lax.scan(
        edge_block,
        start_sum,
        (edge_blocks, source_blocks, target_blocks, jnp.arange(block_count, dtype=jnp.int32)),
    )
    agg_pair = agg_pair.astype(jnp.bfloat16)
    agg = agg_pair[:, :width]
    agg_tan = agg_pair[:, width:]
    first, first_tan = jax.jvp(
        lambda a, b: node_update(a, b, node_first, node_second),
        (node_latent, agg),
        (node_tangent, agg_tan),
    )
    first_pair = jnp.concatenate([first, first_tan], axis=1)
    valid = (jnp.arange(slots) < node_counts[0])[:, None]
    masked = jnp.where(valid, first_pair, jnp.zeros_like(first_pair))
    owner = coarse_owner[0]
    weights = (message_first, message_second, coarse_first, coarse_second)
    owned = coarse_source.shape[0]
    rows = jnp.arange(owned * lax.axis_size("grp"))
    selector = (owner[None, :] == rows[:, None]).astype(jnp.bfloat16)
    own_sum = sum_at_owner(
        jnp.dot(selector, masked, preferred_element_type=jnp.float32).astype(jnp.bfloat16), "grp", 0
    )
    mine = own_sum.astype(jnp.bfloat16)
    coarse = gathered_copies(mine, "grp", 0)
    row_nodes = coarse.shape[0]
    three_rows = extended(coarse[None], (("dom", 0),), 1).reshape(3 * row_nodes, 2 * width)
    updated, updated_tan = jax.jvp(
        lambda a, b: coarse_update(a, coarse_source, b, weights),
        (three_rows[:, :width], mine[:, :width]),
        (three_rows[:, width:], mine[:, width:]),
    )
    updated_pair = jnp.concatenate([updated, updated_tan], axis=1)
    piece = gathered_copies(updated_pair, "grp", 0)
    rows = jnp.arange(piece.shape[0])
    selector = (owner[:, None] == rows[None, :]).astype(jnp.bfloat16)
    brought = jnp.dot(selector, piece, preferred_element_type=jnp.float32).astype(jnp.bfloat16)
    final, final_tan = jax.jvp(
        lambda a, b: node_update(a, b, prolong_first, prolong_second),
        (first, brought[:, :width]),
        (first_tan, brought[:, width:]),
    )
    node_output = jnp.where(valid, final, jnp.zeros_like(final))
    tangent_output = jnp.where(valid, final_tan, jnp.zeros_like(final_tan))
    return (node_output, tangent_output)


def solution(mesh):
    in_specs = (
        P(("dom", "grp"), None),
        P(("dom", "grp"), None),
        P(("dom", "grp"), None),
        P(("dom", "grp")),
        P(("dom", "grp")),
        P(("dom", "grp"), None, None),
        P(("dom", "grp"), None),
        P(("dom", "grp"), None),
        P(("dom", "grp"), None),
        P(("dom", "grp"), None),
        P(),
        P(),
        P(),
        P(),
        P(),
        P(),
        P(),
        P(),
        P(),
        P(),
    )
    out_specs = (P(("dom", "grp"), None), P(("dom", "grp"), None))
    return jax.shard_map(
        per_device, mesh=mesh, in_specs=in_specs, out_specs=out_specs, check_vma=False
    )
```

profile of v0, /device:TPU:97, one launch (start us, length us, event | category | flops | bytes accessed | tf_op | source)
XLA Modules:
  0.0 181.8 jit_solution(3300505138562237629)
XLA Ops:
  4.8 5.3 %collective-permute-start = (bf16[128,256]{1,0:T(8,128)(2,1)S(1)}, bf16[128,256]{1,0:T(8,128)(2,1)S(1)}, u32[]{:S(2)}, u32[]{:S(2)}) collective-permute-start(bf16[128,256]{1,0:T(8,128)(2,1)S(1)} %get-tuple-element.168), channel_id=1, source_target_pairs={{0,16},{16,32},{32,48},{48,64},{64,80},{80,96},{96,112},{112,128},... | collective-permute-start | bytes 196616 | tf_op jit(solution)/shard_map/ppermute | solution.py:12
  12.0 3.1 %collective-permute-start.2 = (bf16[128,256]{1,0:T(8,128)(2,1)S(1)}, bf16[128,256]{1,0:T(8,128)(2,1)S(1)}, u32[]{:S(2)}, u32[]{:S(2)}) collective-permute-start(bf16[128,256]{1,0:T(8,128)(2,1)S(1)} %get-tuple-element.166), channel_id=1, source_target_pairs={{0,1},{1,2},{2,3},{3,4},{4,5},{5,6},{6,7},{7,8},{8,9},{9,10},{10,1... | collective-permute-start | bytes 196616 | tf_op jit(solution)/shard_map/ppermute | solution.py:12
  21.9 94.1 %while.11 = (s32[]{:T(128)}, f32[1024,256]{1,0:T(8,128)S(1)}, s32[8,512]{1,0:T(8,128)S(1)}, s32[8]{0:T(128)S(1)}, s32[]{:T(128)}, /*index=5*/bf16[8,512,128]{2,1...) while((s32[]{:T(128)}, f32[1024,256]{1,0:T(8,128)S(1)}, ...), condition=%wide.region_5.6_spmd.clone, body=%wide.region_0.5_spmd.clone.sunk | while | flops 1082133504 | bytes 9884903 | solution.py:159
  22.6 2.1 %fusion.230 = bf16[512,256]{0,1:T(8,128)(2,1)S(1)} fusion(bf16[1536,256]{1,0:T(8,128)(2,1)} %get-tuple-element.335, s32[512]{0:T(512)S(1)} %bitcast.93), kind=kOutput, calls=%fused_computation.10.clone.1 | convolution fusion | flops 403570688 | bytes 1050624 | tf_op jit(solution)/shard_map/while/body/eval_jaxpr/dot_general | solution.py:95
  25.8 2.0 %fusion.232 = f32[512,128]{1,0:T(8,128)} fusion(bf16[384,128]{1,0:T(8,128)(2,1)} %get-tuple-element.337, bf16[512,128]{0,1:T(8,128)(2,1)S(1)} %get-tuple-element.281, bf16[512,128]{0,1:T(8,128)(2,1)S(1)} %get-tuple-element.283, bf16[512,128]{0,1:T(8,128)(2,1)S(1)} %bitcast.81), kind=kOutput, calls=%fused_computation.13.clone.1 | convolution fusion | flops 51511296 | bytes 753664 | tf_op jit(solution)/shard_map/while/body/eval_jaxpr/jvp()/dot_general | solution.py:62
  34.4 2.1 %fusion.230 = bf16[512,256]{0,1:T(8,128)(2,1)S(1)} fusion(bf16[1536,256]{1,0:T(8,128)(2,1)} %get-tuple-element.335, s32[512]{0:T(512)S(1)} %bitcast.93), kind=kOutput, calls=%fused_computation.10.clone.1 | convolution fusion | flops 403570688 | bytes 1050624 | tf_op jit(solution)/shard_map/while/body/eval_jaxpr/dot_general | solution.py:95
  37.6 2.0 %fusion.232 = f32[512,128]{1,0:T(8,128)} fusion(bf16[384,128]{1,0:T(8,128)(2,1)} %get-tuple-element.337, bf16[512,128]{0,1:T(8,128)(2,1)S(1)} %get-tuple-element.281, bf16[512,128]{0,1:T(8,128)(2,1)S(1)} %get-tuple-element.283, bf16[512,128]{0,1:T(8,128)(2,1)S(1)} %bitcast.81), kind=kOutput, calls=%fused_computation.13.clone.1 | convolution fusion | flops 51511296 | bytes 753664 | tf_op jit(solution)/shard_map/while/body/eval_jaxpr/jvp()/dot_general | solution.py:62
  46.2 2.1 %fusion.230 = bf16[512,256]{0,1:T(8,128)(2,1)S(1)} fusion(bf16[1536,256]{1,0:T(8,128)(2,1)} %get-tuple-element.335, s32[512]{0:T(512)S(1)} %bitcast.93), kind=kOutput, calls=%fused_computation.10.clone.1 | convolution fusion | flops 403570688 | bytes 1050624 | tf_op jit(solution)/shard_map/while/body/eval_jaxpr/dot_general | solution.py:95
  49.3 2.0 %fusion.232 = f32[512,128]{1,0:T(8,128)} fusion(bf16[384,128]{1,0:T(8,128)(2,1)} %get-tuple-element.337, bf16[512,128]{0,1:T(8,128)(2,1)S(1)} %get-tuple-element.281, bf16[512,128]{0,1:T(8,128)(2,1)S(1)} %get-tuple-element.283, bf16[512,128]{0,1:T(8,128)(2,1)S(1)} %bitcast.81), kind=kOutput, calls=%fused_computation.13.clone.1 | convolution fusion | flops 51511296 | bytes 753664 | tf_op jit(solution)/shard_map/while/body/eval_jaxpr/jvp()/dot_general | solution.py:62
  57.9 2.1 %fusion.230 = bf16[512,256]{0,1:T(8,128)(2,1)S(1)} fusion(bf16[1536,256]{1,0:T(8,128)(2,1)} %get-tuple-element.335, s32[512]{0:T(512)S(1)} %bitcast.93), kind=kOutput, calls=%fused_computation.10.clone.1 | convolution fusion | flops 403570688 | bytes 1050624 | tf_op jit(solution)/shard_map/while/body/eval_jaxpr/dot_general | solution.py:95
  61.1 2.0 %fusion.232 = f32[512,128]{1,0:T(8,128)} fusion(bf16[384,128]{1,0:T(8,128)(2,1)} %get-tuple-element.337, bf16[512,128]{0,1:T(8,128)(2,1)S(1)} %get-tuple-element.281, bf16[512,128]{0,1:T(8,128)(2,1)S(1)} %get-tuple-element.283, bf16[512,128]{0,1:T(8,128)(2,1)S(1)} %bitcast.81), kind=kOutput, calls=%fused_computation.13.clone.1 | convolution fusion | flops 51511296 | bytes 753664 | tf_op jit(solution)/shard_map/while/body/eval_jaxpr/jvp()/dot_general | solution.py:62
  69.7 2.1 %fusion.230 = bf16[512,256]{0,1:T(8,128)(2,1)S(1)} fusion(bf16[1536,256]{1,0:T(8,128)(2,1)} %get-tuple-element.335, s32[512]{0:T(512)S(1)} %bitcast.93), kind=kOutput, calls=%fused_computation.10.clone.1 | convolution fusion | flops 403570688 | bytes 1050624 | tf_op jit(solution)/shard_map/while/body/eval_jaxpr/dot_general | solution.py:95
  72.9 2.0 %fusion.232 = f32[512,128]{1,0:T(8,128)} fusion(bf16[384,128]{1,0:T(8,128)(2,1)} %get-tuple-element.337, bf16[512,128]{0,1:T(8,128)(2,1)S(1)} %get-tuple-element.281, bf16[512,128]{0,1:T(8,128)(2,1)S(1)} %get-tuple-element.283, bf16[512,128]{0,1:T(8,128)(2,1)S(1)} %bitcast.81), kind=kOutput, calls=%fused_computation.13.clone.1 | convolution fusion | flops 51511296 | bytes 753664 | tf_op jit(solution)/shard_map/while/body/eval_jaxpr/jvp()/dot_general | solution.py:62
  81.5 2.1 %fusion.230 = bf16[512,256]{0,1:T(8,128)(2,1)S(1)} fusion(bf16[1536,256]{1,0:T(8,128)(2,1)} %get-tuple-element.335, s32[512]{0:T(512)S(1)} %bitcast.93), kind=kOutput, calls=%fused_computation.10.clone.1 | convolution fusion | flops 403570688 | bytes 1050624 | tf_op jit(solution)/shard_map/while/body/eval_jaxpr/dot_general | solution.py:95
  84.6 2.0 %fusion.232 = f32[512,128]{1,0:T(8,128)} fusion(bf16[384,128]{1,0:T(8,128)(2,1)} %get-tuple-element.337, bf16[512,128]{0,1:T(8,128)(2,1)S(1)} %get-tuple-element.281, bf16[512,128]{0,1:T(8,128)(2,1)S(1)} %get-tuple-element.283, bf16[512,128]{0,1:T(8,128)(2,1)S(1)} %bitcast.81), kind=kOutput, calls=%fused_computation.13.clone.1 | convolution fusion | flops 51511296 | bytes 753664 | tf_op jit(solution)/shard_map/while/body/eval_jaxpr/jvp()/dot_general | solution.py:62
  93.2 2.1 %fusion.230 = bf16[512,256]{0,1:T(8,128)(2,1)S(1)} fusion(bf16[1536,256]{1,0:T(8,128)(2,1)} %get-tuple-element.335, s32[512]{0:T(512)S(1)} %bitcast.93), kind=kOutput, calls=%fused_computation.10.clone.1 | convolution fusion | flops 403570688 | bytes 1050624 | tf_op jit(solution)/shard_map/while/body/eval_jaxpr/dot_general | solution.py:95
  105.0 2.1 %fusion.230 = bf16[512,256]{0,1:T(8,128)(2,1)S(1)} fusion(bf16[1536,256]{1,0:T(8,128)(2,1)} %get-tuple-element.335, s32[512]{0:T(512)S(1)} %bitcast.93), kind=kOutput, calls=%fused_computation.10.clone.1 | convolution fusion | flops 403570688 | bytes 1050624 | tf_op jit(solution)/shard_map/while/body/eval_jaxpr/dot_general | solution.py:95
  108.1 2.0 %fusion.232 = f32[512,128]{1,0:T(8,128)} fusion(bf16[384,128]{1,0:T(8,128)(2,1)} %get-tuple-element.337, bf16[512,128]{0,1:T(8,128)(2,1)S(1)} %get-tuple-element.281, bf16[512,128]{0,1:T(8,128)(2,1)S(1)} %get-tuple-element.283, bf16[512,128]{0,1:T(8,128)(2,1)S(1)} %bitcast.81), kind=kOutput, calls=%fused_computation.13.clone.1 | convolution fusion | flops 51511296 | bytes 753664 | tf_op jit(solution)/shard_map/while/body/eval_jaxpr/jvp()/dot_general | solution.py:62
  119.1 15.6 %all_to_all.15 = bf16[16,32,256]{2,1,0:T(8,128)(2,1)S(1)} all-to-all(bf16[16,32,256]{2,1,0:T(8,128)(2,1)S(1)} %bitcast.89), channel_id=1, replica_groups=mesh['dom'=16,'grp'=16] {'grp'}, dimensions={0} | all-to-all | bytes 524288 | tf_op jit(solution)/shard_map/all_to_all | solution.py:23
  135.5 3.5 %all-to-all-start.1 = ((bf16[16,32,256]{2,1,0:T(8,128)(2,1)}), bf16[16,32,256]{2,1,0:T(8,128)(2,1)S(1)}, u32[]{:S(2)}, u32[]{:S(2)}) async-start(bf16[16,32,256]{2,1,0:T(8,128)(2,1)} %broadcast_in_dim.51), calls=%async_computation.1 | async-start | bytes 524288 | tf_op jit(solution)/shard_map/all_to_all | solution.py:35
  139.2 7.3 %all-to-all-done.1 = bf16[16,32,256]{2,1,0:T(8,128)(2,1)S(1)} async-done(((bf16[16,32,256]{2,1,0:T(8,128)(2,1)}), bf16[16,32,256]{2,1,0:T(8,128)(2,1)S(1)}, u32[]{:S(2)}, u32[]{:S(2)}) %all-to-all-start.1) | async-done | bytes 262176 | tf_op jit(solution)/shard_map/all_to_all | solution.py:35
  146.5 7.8 %collective-permute-start.4 = (bf16[1,512,256]{2,1,0:T(8,128)(2,1)S(1)}, bf16[1,512,256]{2,1,0:T(8,128)(2,1)S(1)}, u32[]{:S(2)}, u32[]{:S(2)}) collective-permute-start(bf16[1,512,256]{2,1,0:T(8,128)(2,1)S(1)} %bitcast.83), channel_id=1, source_target_pairs={{0,16},{16,32},{32,48},{48,64},{64,80},{80,96},{96,112},{112,128},... | collective-permute-start | bytes 786440 | tf_op jit(solution)/shard_map/ppermute | solution.py:49
  157.6 5.6 %collective-permute-done.5 = bf16[1,512,256]{2,1,0:T(8,128)(2,1)S(1)} collective-permute-done((bf16[1,512,256]{2,1,0:T(8,128)(2,1)S(1)}, bf16[1,512,256]{2,1,0:T(8,128)(2,1)S(1)}, u32[]{:S(2)}, u32[]{:S(2)}) %collective-permute-start.5) | collective-permute-done | bytes 262176 | tf_op jit(solution)/shard_map/ppermute | solution.py:50
  167.1 10.2 %all_to_all.16 = bf16[16,32,256]{2,1,0:T(8,128)(2,1)S(1)} all-to-all(bf16[16,32,256]{2,1,0:T(8,128)(2,1)S(1)} %broadcast_in_dim.55), channel_id=1, replica_groups=mesh['dom'=16,'grp'=16] {'grp'}, dimensions={0} | all-to-all | bytes 524288 | tf_op jit(solution)/shard_map/all_to_all | solution.py:35
  (267 shorter events, 85.1 us)
Async XLA Ops:
  0.6 115.5 %copy-start = (bf16[256,128]{1,0:T(8,128)(2,1)S(1)}, bf16[256,128]{1,0:T(8,128)(2,1)}, u32[]{:S(2)}) copy-start(bf16[256,128]{1,0:T(8,128)(2,1)} %param.34) | copy-start | bytes 196612
  0.6 3.6 %copy-start.16 = (s32[1,4,128]{2,1,0:T(4,128)S(1)}, s32[1,4,128]{2,1,0:T(4,128)}, u32[]{:S(2)}) copy-start(s32[1,4,128]{2,1,0:T(4,128)} %param.27) | copy-start | bytes 6148
  4.2 12.3 %copy-start.1 = (bf16[1024,128]{1,0:T(8,128)(2,1)S(1)}, bf16[1024,128]{1,0:T(8,128)(2,1)}, u32[]{:S(2)}) copy-start(bf16[1024,128]{1,0:T(8,128)(2,1)} %param.22) | copy-start | bytes 786436
  4.2 12.4 %copy-start.2 = (bf16[1024,128]{1,0:T(8,128)(2,1)S(1)}, bf16[1024,128]{1,0:T(8,128)(2,1)}, u32[]{:S(2)}) copy-start(bf16[1024,128]{1,0:T(8,128)(2,1)} %param.23) | copy-start | bytes 786436
  4.7 12.6 %copy-start.6 = (s32[1,4096]{1,0:T(1,128)S(1)}, s32[1,4096]{1,0:T(1,128)}, u32[]{:S(2)}) copy-start(s32[1,4096]{1,0:T(1,128)} %param.29) | copy-start | bytes 49156
  4.7 13.3 %copy-start.7 = (s32[1,4096]{1,0:T(1,128)S(1)}, s32[1,4096]{1,0:T(1,128)}, u32[]{:S(2)}) copy-start(s32[1,4096]{1,0:T(1,128)} %param.28) | copy-start | bytes 49156
  4.7 17.2 %copy-start.10 = (bf16[128,128]{1,0:T(8,128)(2,1)S(1)}, bf16[128,128]{1,0:T(8,128)(2,1)}, u32[]{:S(2)}) copy-start(bf16[128,128]{1,0:T(8,128)(2,1)} %param.33) | copy-start | bytes 98308
  4.8 14.6 %collective-permute-start = (bf16[128,256]{1,0:T(8,128)(2,1)S(1)}, bf16[128,256]{1,0:T(8,128)(2,1)S(1)}, u32[]{:S(2)}, u32[]{:S(2)}) collective-permute-start(bf16[128,256]{1,0:T(8,128)(2,1)S(1)} %get-tuple-element.168), channel_id=1, source_target_pairs={{0,16},{16,32},{32,48},{48,64},{64,80},{80,96},{96,112},{112,128},... | collective-permute-start | bytes 196616 | tf_op jit(solution)/shard_map/ppermute | solution.py:12
  10.1 9.9 %collective-permute-start.1 = (bf16[128,256]{1,0:T(8,128)(2,1)S(1)}, bf16[128,256]{1,0:T(8,128)(2,1)S(1)}, u32[]{:S(2)}, u32[]{:S(2)}) collective-permute-start(bf16[128,256]{1,0:T(8,128)(2,1)S(1)} %get-tuple-element.167), channel_id=1, source_target_pairs={{16,0},{32,16},{48,32},{64,48},{80,64},{96,80},{112,96},{128,112},... | collective-permute-start | bytes 196616 | tf_op jit(solution)/shard_map/ppermute | solution.py:12
  12.0 8.6 %collective-permute-start.2 = (bf16[128,256]{1,0:T(8,128)(2,1)S(1)}, bf16[128,256]{1,0:T(8,128)(2,1)S(1)}, u32[]{:S(2)}, u32[]{:S(2)}) collective-permute-start(bf16[128,256]{1,0:T(8,128)(2,1)S(1)} %get-tuple-element.166), channel_id=1, source_target_pairs={{0,1},{1,2},{2,3},{3,4},{4,5},{5,6},{6,7},{7,8},{8,9},{9,10},{10,1... | collective-permute-start | bytes 196616 | tf_op jit(solution)/shard_map/ppermute | solution.py:12
  15.2 6.1 %collective-permute-start.3 = (bf16[128,256]{1,0:T(8,128)(2,1)S(1)}, bf16[128,256]{1,0:T(8,128)(2,1)S(1)}, u32[]{:S(2)}, u32[]{:S(2)}) collective-permute-start(bf16[128,256]{1,0:T(8,128)(2,1)S(1)} %get-tuple-element.165), channel_id=1, source_target_pairs={{1,0},{2,1},{3,2},{4,3},{5,4},{6,5},{7,6},{8,7},{9,8},{10,9},{11,1... | collective-permute-start | bytes 196616 | tf_op jit(solution)/shard_map/ppermute | solution.py:12
  25.8 2.0 %copy-start.9 = (bf16[384,128]{1,0:T(8,128)(2,1)S(1)}, bf16[384,128]{1,0:T(8,128)(2,1)}, u32[]{:S(2)}) copy-start(bf16[384,128]{1,0:T(8,128)(2,1)} %get-tuple-element.337) | copy-start | bytes 294916 | tf_op jit(solution)/shard_map/while
  37.5 2.0 %copy-start.9 = (bf16[384,128]{1,0:T(8,128)(2,1)S(1)}, bf16[384,128]{1,0:T(8,128)(2,1)}, u32[]{:S(2)}) copy-start(bf16[384,128]{1,0:T(8,128)(2,1)} %get-tuple-element.337) | copy-start | bytes 294916 | tf_op jit(solution)/shard_map/while
  49.3 2.0 %copy-start.9 = (bf16[384,128]{1,0:T(8,128)(2,1)S(1)}, bf16[384,128]{1,0:T(8,128)(2,1)}, u32[]{:S(2)}) copy-start(bf16[384,128]{1,0:T(8,128)(2,1)} %get-tuple-element.337) | copy-start | bytes 294916 | tf_op jit(solution)/shard_map/while
  61.1 2.0 %copy-start.9 = (bf16[384,128]{1,0:T(8,128)(2,1)S(1)}, bf16[384,128]{1,0:T(8,128)(2,1)}, u32[]{:S(2)}) copy-start(bf16[384,128]{1,0:T(8,128)(2,1)} %get-tuple-element.337) | copy-start | bytes 294916 | tf_op jit(solution)/shard_map/while
  72.8 2.0 %copy-start.9 = (bf16[384,128]{1,0:T(8,128)(2,1)S(1)}, bf16[384,128]{1,0:T(8,128)(2,1)}, u32[]{:S(2)}) copy-start(bf16[384,128]{1,0:T(8,128)(2,1)} %get-tuple-element.337) | copy-start | bytes 294916 | tf_op jit(solution)/shard_map/while
  84.6 2.0 %copy-start.9 = (bf16[384,128]{1,0:T(8,128)(2,1)S(1)}, bf16[384,128]{1,0:T(8,128)(2,1)}, u32[]{:S(2)}) copy-start(bf16[384,128]{1,0:T(8,128)(2,1)} %get-tuple-element.337) | copy-start | bytes 294916 | tf_op jit(solution)/shard_map/while
  96.4 2.0 %copy-start.9 = (bf16[384,128]{1,0:T(8,128)(2,1)S(1)}, bf16[384,128]{1,0:T(8,128)(2,1)}, u32[]{:S(2)}) copy-start(bf16[384,128]{1,0:T(8,128)(2,1)} %get-tuple-element.337) | copy-start | bytes 294916 | tf_op jit(solution)/shard_map/while
  108.1 2.0 %copy-start.9 = (bf16[384,128]{1,0:T(8,128)(2,1)S(1)}, bf16[384,128]{1,0:T(8,128)(2,1)}, u32[]{:S(2)}) copy-start(bf16[384,128]{1,0:T(8,128)(2,1)} %get-tuple-element.337) | copy-start | bytes 294916 | tf_op jit(solution)/shard_map/while
  119.1 19.9 %copy-start.8 = (s32[32,8]{0,1:T(8,128)S(1)}, s32[32,8]{0,1:T(8,128)}, u32[]{:S(2)}) copy-start(s32[32,8]{0,1:T(8,128)} %param.31) | copy-start | bytes 3076
  135.5 11.0 %all-to-all-start.1 = ((bf16[16,32,256]{2,1,0:T(8,128)(2,1)}), bf16[16,32,256]{2,1,0:T(8,128)(2,1)S(1)}, u32[]{:S(2)}, u32[]{:S(2)}) async-start(bf16[16,32,256]{2,1,0:T(8,128)(2,1)} %broadcast_in_dim.51), calls=%async_computation.1 | async-start | bytes 524288 | tf_op jit(solution)/shard_map/all_to_all | solution.py:35
  146.5 11.1 %collective-permute-start.4 = (bf16[1,512,256]{2,1,0:T(8,128)(2,1)S(1)}, bf16[1,512,256]{2,1,0:T(8,128)(2,1)S(1)}, u32[]{:S(2)}, u32[]{:S(2)}) collective-permute-start(bf16[1,512,256]{2,1,0:T(8,128)(2,1)S(1)} %bitcast.83), channel_id=1, source_target_pairs={{0,16},{16,32},{32,48},{48,64},{64,80},{80,96},{96,112},{112,128},... | collective-permute-start | bytes 786440 | tf_op jit(solution)/shard_map/ppermute | solution.py:49
  154.3 8.9 %collective-permute-start.5 = (bf16[1,512,256]{2,1,0:T(8,128)(2,1)S(1)}, bf16[1,512,256]{2,1,0:T(8,128)(2,1)S(1)}, u32[]{:S(2)}, u32[]{:S(2)}) collective-permute-start(bf16[1,512,256]{2,1,0:T(8,128)(2,1)S(1)} %bitcast.84), channel_id=1, source_target_pairs={{16,0},{32,16},{48,32},{64,48},{80,64},{96,80},{112,96},{128,112},... | collective-permute-start | bytes 786440 | tf_op jit(solution)/shard_map/ppermute | solution.py:50
  163.4 1.9 %copy-start.12 = (bf16[128,128]{1,0:T(8,128)(2,1)S(1)}, bf16[128,128]{1,0:T(8,128)(2,1)}, u32[]{:S(2)}) copy-start(bf16[128,128]{1,0:T(8,128)(2,1)} %param.37) | copy-start | bytes 98308
  (7 other events, 6.7 us)
where the time goes:
time: 184 us; the launch traced here: 182 us
  matrix products  73.1 us (40%)
  local copies, waits for them, and re-layouts  26.2 us (14%)
  blocking collectives  25.7 us (14%)
  starting transfers between devices  24.9 us (14%)
  waiting for transfers between devices  14.3 us (8%)
  other arithmetic  9.42 us (5%)
  loops' own time  6.23 us (3%)
  between operations  1.84 us (1%)
    dot_general x24, matrix products, perceptron(): return jnp.dot(hidden, second, preferred_element_type=jnp.float32)  24.8 us
    dot_general x9, matrix products, select_rows(): jnp.dot(selector, values, preferred_element_type=jnp.float32)  17 us
    dot_general x12, matrix products, perceptron(): jnp.dot(inputs, first, preferred_element_type=jnp.float32)  16.7 us
    all_to_all x1, blocking collectives, sum_at_owner(): lax.all_to_all(pieces, axis, split_axis=0, concat_axis=0, tiled=True)  15.6 us
    dynamic_slice x32, local copies, waits for them, and re-layouts, per_device(): lax.scan(edge_block, start_sum, (edge_blocks, source_blocks, target_block...  13.1 us
    ppermute x4, starting transfers between devices, from_behind(): return lax.ppermute(x, axis, pairs)  11.6 us
    all_to_all x1, blocking collectives, sent_to_all(): return lax.all_to_all(copies, axis, split_axis=0, concat_axis=0, tiled=True)  10.2 us
    dot_general x8, matrix products, edge_block(): jnp.einsum('es,ef->sf', target_pick, pair, preferred_element_type=jnp.flo...  8.04 us
  transfers between devices with their start and end apart: 7, of which 3 were waited for; matrix products, arithmetic and copies ran while one was open for 2% of the time, Pallas kernels for 0%

commit v1 on v0

v1 whole, which is shorter than its diff:
```python
import functools

import jax
import jax.numpy as jnp
from jax import lax
from jax.experimental import pallas as pl
from jax.experimental.pallas import tpu as pltpu
from jax.sharding import PartitionSpec as P

F32, BF16, I32, I16 = jnp.float32, jnp.bfloat16, jnp.int32, jnp.int16
MESH = pl.DeviceIdType.MESH
L = 128
LANES = 128


def dot(a, b):
    return jnp.dot(a, b, preferred_element_type=F32)


def twice(w):
    w = w.astype(F32)
    z = jnp.zeros_like(w)
    both = jnp.concatenate([jnp.concatenate([w, z], 1), jnp.concatenate([z, w], 1)], 0)
    return both.astype(BF16)


def centred(w):
    w = w.astype(F32)
    return w - jnp.mean(w, axis=-1, keepdims=True)


def swish_pair(pre):
    v, vt = pre[:, :L], pre[:, L:]
    gate = 1.0 / (1.0 + jnp.exp(-v))
    h = v * gate
    ht = vt * (gate + h * (1.0 - gate))
    return jnp.concatenate([h.astype(BF16), ht.astype(BF16)], 1)


def norm_pair(value, mean):
    c, ct = value[:, :L], value[:, L:]
    stats = dot(jnp.concatenate([(c * c).astype(BF16), (c * ct).astype(BF16)], 1), mean)
    r = lax.rsqrt(stats[:, :L] + 1e-5)
    y = c * r
    return y, r * ct - y * (r * r * stats[:, L:])


def column(row, kind):
    return jnp.transpose(jnp.broadcast_to(row, (LANES, LANES))).astype(kind)


def residual(base, y):
    return (base.astype(F32) + y).astype(BF16)


def ring_offsets(ny, nx):
    near = lambda a, n: min(a, n - a)
    pairs = [(a, b) for a in range(ny) for b in range(nx) if (a, b) != (0, 0)]
    return sorted(pairs, key=lambda p: (near(p[0], ny) + near(p[1], nx), p))


def layer_kernel(
    sizes,
    node_count, edge_count,
    latent, tangent, edges_hbm, lists, source, target, owner, coarse_source,
    edge_first, edge_second, node_first, node_second, message_first, message_second, coarse_first, coarse_second,
    first_out, updated_out,
    edges, local, halo_out, halo_in, table, columns, onehot, pick, pre, acc, weights, part, arrived, rows3, node_pair,
    load_sem, halo_send, halo_recv, rs_send, rs_recv, ag_send, ag_recv, side_send, side_recv, fin_send, fin_recv,
):
    n_dom, n_grp, ny, nx = sizes
    slots, rim, edge_slots, own = latent.shape[0], lists.shape[2], source.shape[1], coarse_source.shape[0]
    halo_rows, row_nodes = 4 * rim, own * n_grp
    block = onehot.shape[0]
    blocks = edge_slots // block
    d, g = lax.axis_index("dom"), lax.axis_index("grp")
    y, x = g // nx, g % nx
    offsets = ring_offsets(ny, nx)
    ahead = [((y + a) % ny) * nx + (x + b) % nx for a, b in offsets]
    behind = [((y + ny - a) % ny) * nx + (x + nx - b) % nx for a, b in offsets]
    sides = [(d < n_dom - 1, (d + 1, g)), (d > 0, (d - 1, g)), (g < n_grp - 1, (d, g + 1)), (g > 0, (d, g - 1))]
    origins = [d > 0, d < n_dom - 1, g > 0, g < n_grp - 1]

    def remote(src, dst, send, recv, to):
        return pltpu.make_async_remote_copy(src_ref=src, dst_ref=dst, send_sem=send, recv_sem=recv, device_id=to, device_id_type=MESH)

    load = pltpu.make_async_copy(edges_hbm, edges, load_sem)
    load.start()
    barrier = pltpu.get_barrier_semaphore()
    for k in ahead:
        pl.semaphore_signal(barrier, inc=1, device_id=(d, k), device_id_type=MESH)
    for there, to in sides[:2]:
        @pl.when(there)
        def _():
            pl.semaphore_signal(barrier, inc=1, device_id=to, device_id_type=MESH)

    lanes = lax.broadcasted_iota(I32, (LANES, LANES), 1).astype(I16)
    one, zero = jnp.ones((LANES, LANES), BF16), jnp.zeros((LANES, LANES), BF16)

    def spread(ref, row, col, count, col_at):
        for j in range(count):
            ref[row : row + LANES, col + j * LANES : col + (j + 1) * LANES] = jnp.where(
                col_at == lanes + jnp.array(j * LANES, I16), one, zero
            )

    local[:, :L] = latent[...]
    local[:, L:] = tangent[...]
    for b in range(4):
        spread(onehot, b * rim, 0, slots // LANES, column(lists[0, b : b + 1, :], I16))
    halo_out[...] = dot(onehot[:halo_rows, :slots], local[...]).astype(BF16).reshape(halo_out.shape)

    weights[0] = twice(edge_first[L : 2 * L, :])
    weights[1] = twice(edge_first[2 * L : 3 * L, :])
    weights[2] = twice(centred(edge_second[...]))
    weights[3] = twice(jnp.full((L, L), 1.0 / L, F32))
    mean = weights.at[3]

    for b, (there, to) in enumerate(sides):
        @pl.when(jnp.logical_not(origins[b]))
        def _():
            halo_in[b] = jnp.zeros(halo_in.shape[1:], BF16)

    pl.semaphore_wait(barrier, len(ahead) + jnp.where(d > 0, 1, 0) + jnp.where(d < n_dom - 1, 1, 0))
    halo_copies = [remote(halo_out.at[b], halo_in.at[b], halo_send.at[b], halo_recv.at[b], to) for b, (_, to) in enumerate(sides)]
    for b, (there, _) in enumerate(sides):
        @pl.when(there)
        def _():
            halo_copies[b].start()

    table[:slots, :] = dot(local[...], weights[0]).astype(BF16)
    table[slots : 2 * slots, :] = dot(local[...], weights[1]).astype(BF16)
    load.wait()

    def gather_local(i, _):
        at = pl.multiple_of(i * block, block)
        for q in range(block // LANES):
            here = pl.multiple_of(at + q * LANES, LANES)
            s = column(source[0:1, pl.ds(here, LANES)], I16)
            t = column(target[0:1, pl.ds(here, LANES)], I16)
            columns[pl.ds(here, LANES), :] = s
            spread(onehot, q * LANES, 0, slots // LANES, s)
            spread(onehot, q * LANES, slots, slots // LANES, t)
        out = dot(onehot[...], table[: 2 * slots, :])
        pre[pl.ds(at, block), :L] = out[:, :L] + dot(edges[pl.ds(at, block), :], edge_first[:L, :])
        pre[pl.ds(at, block), L:] = out[:, L:]
        return 0

    lax.fori_loop(0, blocks, gather_local, 0)

    for b, there in enumerate(origins):
        @pl.when(there)
        def _():
            halo_copies[b].wait_recv()
    table[2 * slots :, :] = dot(halo_in[...].reshape(halo_rows, 2 * L), weights[0]).astype(BF16)
    acc[...] = jnp.zeros_like(acc)
    total = edge_count[0]
    rows_at = lax.broadcasted_iota(I32, (LANES, block), 0).astype(I16)
    one_b, zero_b = jnp.ones((LANES, block), BF16), jnp.zeros((LANES, block), BF16)

    def edge_block(i, _):
        at = pl.multiple_of(i * block, block)
        for q in range(block // LANES):
            s = columns[pl.ds(pl.multiple_of(at + q * LANES, LANES), LANES), :]
            spread(onehot, q * LANES, 0, halo_rows // LANES, s - jnp.array(slots, I16))
        hidden = swish_pair(pre[pl.ds(at, block), :] + dot(onehot[:, :halo_rows], table[2 * slots :, :]))
        up, up_tan = norm_pair(dot(hidden, weights[2]), mean[...])
        pair = jnp.concatenate([residual(edges[pl.ds(at, block), :], up), up_tan.astype(BF16)], 1)
        ids = at + lax.broadcasted_iota(I32, (1, block), 1)
        live = jnp.where(ids < total, target[0:1, pl.ds(at, block)], -1)
        live = jnp.broadcast_to(live, (LANES, block)).astype(I16)
        for j in range(slots // LANES):
            pick[j * LANES : (j + 1) * LANES, :] = jnp.where(live == rows_at + jnp.array(j * LANES, I16), one_b, zero_b)
        acc[...] += dot(pick[...], pair)
        return 0

    lax.fori_loop(0, blocks, edge_block, 0)

    weights[0] = twice(node_first[:L, :])
    weights[1] = twice(node_first[L:, :])
    weights[2] = twice(centred(node_second[...]))
    hidden = swish_pair(dot(local[...], weights[0]) + dot(acc[...].astype(BF16), weights[1]))
    up, up_tan = norm_pair(dot(hidden, weights[2]), mean[...])
    node_pair[:, :L] = residual(latent[...], up)
    node_pair[:, L:] = residual(tangent[...], up_tan)
    first_out[...] = node_pair[...]

    ids = lax.broadcasted_iota(I32, (1, slots), 1)
    live = jnp.where(ids < node_count[0], owner[...], -1)
    live = jnp.broadcast_to(live, (LANES, slots)).astype(I16)
    rows_n = lax.broadcasted_iota(I32, (LANES, slots), 0).astype(I16)
    one_n, zero_n = jnp.ones((LANES, slots), BF16), jnp.zeros((LANES, slots), BF16)
    for j in range(row_nodes // LANES):
        onehot[j * LANES : (j + 1) * LANES, :slots] = jnp.where(live == rows_n + jnp.array(j * LANES, I16), one_n, zero_n)
    part[...] = dot(onehot[:row_nodes, :slots], node_pair[...]).astype(BF16).reshape(part.shape)

    n = len(offsets)
    rs = [remote(part.at[ahead[m]], arrived.at[m], rs_send.at[m], rs_recv.at[m], (d, ahead[m])) for m in range(n)]
    for m in reversed(range(n)):
        rs[m].start()
    weights[0] = twice(message_first[:L, :])
    weights[1] = twice(message_first[L:, :])
    weights[2] = twice(message_second[...])
    weights[4] = twice(coarse_first[:L, :])
    weights[5] = twice(coarse_first[L:, :])
    weights[6] = twice(centred(coarse_second[...]))
    for j in range(coarse_source.shape[1]):
        ids = lax.broadcasted_iota(I32, (own, 3 * row_nodes), 1)
        onehot[j * own : (j + 1) * own, : 3 * row_nodes] = jnp.where(coarse_source[:, j : j + 1] == ids, 1.0, 0.0).astype(BF16)
    for beyond, slot in ((d == 0, 0), (d == n_dom - 1, 2)):
        @pl.when(beyond)
        def _():
            rows3[slot] = jnp.zeros(rows3.shape[1:], BF16)

    mine = part[g].astype(F32)
    for m in range(n):
        rs[m].wait_recv()
        mine = mine + arrived[m].astype(F32)
    mine = mine.astype(BF16)
    rows3[1, g] = mine

    ag = [remote(rows3.at[1, g], rows3.at[1, g], ag_send.at[m], ag_recv.at[m], (d, ahead[m])) for m in range(n)]
    for m in reversed(range(n)):
        ag[m].start()

    def passed_on(k, m):
        up = remote(rows3.at[1, k], rows3.at[0, k], side_send.at[0, m], side_recv.at[0, m], (d + 1, g))
        down = remote(rows3.at[1, k], rows3.at[2, k], side_send.at[1, m], side_recv.at[1, m], (d - 1, g))
        return up, down

    forwards = [passed_on(g, n)] + [passed_on(behind[m], m) for m in range(n)]
    for m in range(-1, n):
        if m >= 0:
            remote(rows3.at[1, behind[m]], rows3.at[1, behind[m]], ag_send.at[m], ag_recv.at[m], (d, ahead[m])).wait_recv()
        up, down = forwards[m + 1]
        @pl.when(d < n_dom - 1)
        def _():
            up.start()
        @pl.when(d > 0)
        def _():
            down.start()
    senders = dot(onehot[: own * 8, row_nodes : 2 * row_nodes], rows3[1].reshape(row_nodes, 2 * L))
    receiver = dot(mine, weights[1])
    for m in range(n + 1):
        k = g if m == 0 else behind[m - 1]
        i = n if m == 0 else m - 1
        @pl.when(d > 0)
        def _():
            remote(rows3.at[1, k], rows3.at[0, k], side_send.at[0, i], side_recv.at[0, i], (d + 1, g)).wait_recv()
        @pl.when(d < n_dom - 1)
        def _():
            remote(rows3.at[1, k], rows3.at[2, k], side_send.at[1, i], side_recv.at[1, i], (d - 1, g)).wait_recv()
    senders = senders + dot(onehot[: own * 8, :row_nodes], rows3[0].reshape(row_nodes, 2 * L))
    senders = senders + dot(onehot[: own * 8, 2 * row_nodes : 3 * row_nodes], rows3[2].reshape(row_nodes, 2 * L))
    to_all = jnp.concatenate([receiver] * 8, 0)
    hidden = swish_pair(dot(senders.astype(BF16), weights[0]) + to_all)
    terms = dot(hidden, weights[2])
    message = terms[:own]
    for j in range(1, 8):
        message = message + terms[j * own : (j + 1) * own]
    hidden = swish_pair(dot(mine, weights[4]) + dot(message.astype(BF16), weights[5]))
    up, up_tan = norm_pair(dot(hidden, weights[6]), mean[...])
    updated_out[g] = jnp.concatenate([up.astype(BF16), up_tan.astype(BF16)], 1)
    fin = [remote(updated_out.at[g], updated_out.at[g], fin_send.at[m], fin_recv.at[m], (d, ahead[m])) for m in range(n)]
    for m in reversed(range(n)):
        fin[m].start()

    for b, (there, _) in enumerate(sides):
        @pl.when(there)
        def _():
            halo_copies[b].wait_send()
    for m in range(n):
        rs[m].wait_send()
        ag[m].wait_send()
    for up, down in forwards:
        @pl.when(d < n_dom - 1)
        def _():
            up.wait_send()
        @pl.when(d > 0)
        def _():
            down.wait_send()
    for m in range(n):
        fin[m].wait_send()
        remote(updated_out.at[behind[m]], updated_out.at[behind[m]], fin_send.at[m], fin_recv.at[m], (d, ahead[m])).wait_recv()


def final_kernel(node_count, first, updated, owner, prolong_first, prolong_second, node_output, tangent_output, onehot):
    slots, row_nodes = first.shape[0], updated.shape[0]
    lanes = lax.broadcasted_iota(I32, (LANES, LANES), 1).astype(I16)
    one, zero = jnp.ones((LANES, LANES), BF16), jnp.zeros((LANES, LANES), BF16)
    for q in range(slots // LANES):
        at = column(owner[0:1, q * LANES : (q + 1) * LANES], I16)
        for j in range(row_nodes // LANES):
            onehot[q * LANES : (q + 1) * LANES, j * LANES : (j + 1) * LANES] = jnp.where(at == lanes + jnp.array(j * LANES, I16), one, zero)
    brought = dot(onehot[...], updated[...]).astype(BF16)
    mean = twice(jnp.full((L, L), 1.0 / L, F32))
    pair = first[...]
    hidden = swish_pair(dot(pair, twice(prolong_first[:L, :])) + dot(brought, twice(prolong_first[L:, :])))
    up, up_tan = norm_pair(dot(hidden, twice(centred(prolong_second[...]))), mean)
    valid = lax.broadcasted_iota(I32, (slots, L), 0) < node_count[0]
    node_output[...] = jnp.where(valid, pair[:, :L].astype(F32) + up, 0.0).astype(BF16)
    tangent_output[...] = jnp.where(valid, pair[:, L:].astype(F32) + up_tan, 0.0).astype(BF16)


def per_device(
    sizes,
    node_latent, node_tangent, edge_latent, node_counts, edge_counts, send_lists, edge_source, edge_target, coarse_owner, coarse_source,
    edge_first, edge_second, node_first, node_second, message_first, message_second, coarse_first, coarse_second, prolong_first, prolong_second,
):
    n_dom, n_grp, ny, nx = sizes
    slots, edge_slots, rim, own = node_latent.shape[0], edge_latent.shape[0], send_lists.shape[2], coarse_source.shape[0]
    block = 1024
    vmem = pl.BlockSpec(memory_space=pltpu.VMEM)
    smem = pl.BlockSpec(memory_space=pltpu.SMEM)
    others = n_grp - 1
    dma = pltpu.SemaphoreType.DMA
    first, updated = pl.pallas_call(
        functools.partial(layer_kernel, sizes),
        out_shape=(jax.ShapeDtypeStruct((slots, 2 * L), BF16), jax.ShapeDtypeStruct((n_grp, own, 2 * L), BF16)),
        in_specs=[smem, smem, vmem, vmem, pl.BlockSpec(memory_space=pl.ANY)] + [vmem] * 13,
        out_specs=(vmem, vmem),
        scratch_shapes=[
            pltpu.VMEM((edge_slots, L), BF16),
            pltpu.VMEM((slots, 2 * L), BF16),
            pltpu.VMEM((4, rim, 2 * L), BF16),
            pltpu.VMEM((4, rim, 2 * L), BF16),
            pltpu.VMEM((2 * slots + 4 * rim, 2 * L), BF16),
            pltpu.VMEM((edge_slots, LANES), I16),
            pltpu.VMEM((block, 2 * slots), BF16),
            pltpu.VMEM((slots, block), BF16),
            pltpu.VMEM((edge_slots, 2 * L), F32),
            pltpu.VMEM((slots, 2 * L), F32),
            pltpu.VMEM((7, 2 * L, 2 * L), BF16),
            pltpu.VMEM((n_grp, own, 2 * L), BF16),
            pltpu.VMEM((others, own, 2 * L), BF16),
            pltpu.VMEM((3, n_grp, own, 2 * L), BF16),
            pltpu.VMEM((slots, 2 * L), BF16),
            dma(()), dma((4,)), dma((4,)), dma((others,)), dma((others,)), dma((others,)), dma((others,)),
            dma((2, n_grp)), dma((2, n_grp)), dma((others,)), dma((others,)),
        ],
        compiler_params=pltpu.CompilerParams(collective_id=0, has_side_effects=True, vmem_limit_bytes=56 << 20),
    )(
        node_counts, edge_counts, node_latent, node_tangent, edge_latent, send_lists, edge_source, edge_target, coarse_owner, coarse_source,
        edge_first, edge_second, node_first, node_second, message_first, message_second, coarse_first, coarse_second,
    )
    out = jax.ShapeDtypeStruct((slots, L), BF16)
    return pl.pallas_call(
        final_kernel,
        out_shape=(out, out),
        in_specs=[smem] + [vmem] * 5,
        out_specs=(vmem, vmem),
        scratch_shapes=[pltpu.VMEM((slots, own * n_grp), BF16)],
    )(node_counts, first, updated.reshape(n_grp * own, 2 * L), coarse_owner, prolong_first, prolong_second)


def solution(mesh):
    n_dom, n_grp = mesh.shape["dom"], mesh.shape["grp"]
    nx = 4 if n_grp % 4 == 0 and n_grp > 4 else 2
    both = ("dom", "grp")
    rows = P(both, None)
    in_specs = (rows, rows, rows, P(both), P(both), P(both, None, None), rows, rows, rows, rows) + (P(),) * 10
    return jax.shard_map(
        functools.partial(per_device, (n_dom, n_grp, n_grp // nx, nx)),
        mesh=mesh, in_specs=in_specs, out_specs=(rows, rows), check_vma=False,
    )
```

time: 184 us -> 57.4 us (0.31)
  the two profiles are of different devices: /device:TPU:97 before, /device:TPU:1 now
where the time goes in v1:
time: 57.4 us; the launch traced here: 56.8 us
  Pallas kernels  53.5 us (93%)
  between operations  1.93 us (3%)
  local copies, waits for them, and re-layouts  1.37 us (2%)
    pallas_call x1, Pallas kernels, per_device(): pl.pallas_call(functools.partial(layer_kernel, sizes), out_shape=(jax.Sha...  50.1 us
    pallas_call x1, Pallas kernels, per_device(): pl.pallas_call(final_kernel, out_shape=(out, out), in_specs=[smem] + [vme...  3.44 us
    unnamed x1, local copies, waits for them, and re-layouts  1.37 us

profile of v1, /device:TPU:1, one launch (start us, length us, event | category | flops | bytes accessed | tf_op | source)
XLA Modules:
  0.0 56.8 jit_solution(11640014080568212702)
XLA Ops:
  1.9 1.4 %copy.22.coarse_source = s32[32,8]{1,0:T(8,128)} copy(s32[32,8]{0,1:T(8,128)} %param.29) | data formatting | bytes 2048 | tf_op args[9]
  3.3 50.1 %shard_map.203 = (bf16[1024,256]{1,0:T(8,128)(2,1)}, bf16[16,32,256]{2,1,0:T(8,128)(2,1)}) custom-call(s32[1]{0:T(128)S(6)} %copy.23.node_count, s32[1]{0:T(128)S(6)} %copy.24.edge_count, bf16[1024,128]{1,0:T(8,128)(2,1)} %latent.1, bf16[1024,128]{1,0:T(8,128)(2,1)} %tangent.1, bf16[4096,128]{1,0:T(8,128)(2,1)} %edges_hbm.1, s32[1,4,128]{2,1,0:T(4,128)} %lists.1, ...), custom_call_target="tpu_custom_call" | custom-call | tf_op jit(solution)/shard_map/pallas_call | solution.py:316
  53.4 3.4 %shard_map.204 = (bf16[1024,128]{1,0:T(8,128)(2,1)}, bf16[1024,128]{1,0:T(8,128)(2,1)}) custom-call(s32[1]{0:T(128)S(6)} %copy.23.node_count, bf16[1024,256]{1,0:T(8,128)(2,1)} %get-tuple-element.4.first, bf16[512,256]{1,0:T(8,128)(2,1)} %bitcast.1, s32[1,1024]{1,0:T(1,128)} %owner.3, bf16[256,128]{1,0:T(8,128)(2,1)} %prolong_first.1, ...), custom_call_target="tpu_custom_call" | custom-call | tf_op jit(solution)/shard_map/pallas_call | solution.py:346

commit v2 on v1

v2 whole, which is shorter than its diff:
```python
import functools

import jax
import jax.numpy as jnp
from jax import lax
from jax.experimental import pallas as pl
from jax.experimental.pallas import tpu as pltpu
from jax.sharding import PartitionSpec as P

F32, BF16, I32, I16 = jnp.float32, jnp.bfloat16, jnp.int32, jnp.int16
MESH = pl.DeviceIdType.MESH
L = 128
LANES = 128
BLOCK = 1024
NAMES = (
    "node_latent", "node_tangent", "edge_latent", "send_lists", "edge_source", "edge_target",
    "coarse_owner", "coarse_source", "edge_first", "edge_second", "node_first", "node_second", "message_first", "message_second",
    "coarse_first", "coarse_second", "prolong_first", "prolong_second",
)


def dot(a, b):
    return jnp.dot(a, b, preferred_element_type=F32)


def twice(w):
    w = w.astype(F32)
    z = jnp.zeros_like(w)
    both = jnp.concatenate([jnp.concatenate([w, z], 1), jnp.concatenate([z, w], 1)], 0)
    return both.astype(BF16)


def centred(w):
    w = w.astype(F32)
    return w - jnp.mean(w, axis=-1, keepdims=True)


def swish_pair(pre):
    v, vt = pre[:, :L], pre[:, L:]
    gate = 1.0 / (1.0 + jnp.exp(-v))
    h = v * gate
    ht = vt * (gate + h * (1.0 - gate))
    return jnp.concatenate([h.astype(BF16), ht.astype(BF16)], 1)


def norm_pair(value, mean):
    c, ct = value[:, :L], value[:, L:]
    stats = dot(jnp.concatenate([(c * c).astype(BF16), (c * ct).astype(BF16)], 1), mean)
    r = lax.rsqrt(stats[:, :L] + 1e-5)
    y = c * r
    return y, r * ct - y * (r * r * stats[:, L:])


def column(row):
    return jnp.transpose(jnp.broadcast_to(row, (LANES, LANES))).astype(I16)


def iota(shape, axis):
    return lax.broadcasted_iota(I32, shape, axis).astype(I16)


def chosen(hit):
    return jnp.where(hit, jnp.ones(hit.shape, BF16), jnp.zeros(hit.shape, BF16))


def picks(col, count, start=0):
    return chosen(jnp.concatenate([col] * (count // LANES), 1) == iota((col.shape[0], count), 1) + jnp.array(start, I16))


def picks_down(row, count, start=0):
    shape = (count, row.shape[1])
    return chosen(jnp.broadcast_to(row, shape).astype(I16) == iota(shape, 0) + jnp.array(start, I16))


def residual(base, y):
    return (base.astype(F32) + y).astype(BF16)


def ring_offsets(ny, nx):
    near = lambda a, n: min(a, n - a)
    pairs = [(a, b) for a in range(ny) for b in range(nx) if (a, b) != (0, 0)]
    return sorted(pairs, key=lambda p: (near(p[0], ny) + near(p[1], nx), p))


def layer_kernel(sizes, *refs):
    n_dom, n_grp, ny, nx = sizes
    node_count, edge_count = refs[0][0], refs[1][0]
    hbm = dict(zip(NAMES, refs[2:20]))
    (
        node_output, tangent_output,
        local, edges, lists, source, target, owner, coarse_source,
        edge_first, edge_second, node_first, node_second, message_first, message_second, coarse_first, coarse_second, prolong_first, prolong_second,
        halo_out, halo_in, table, columns, pre, pairs, picked, picked_senders, base, weights, part, arrived, rows3, updated, turned, agg,
        load_sem, halo_send, halo_recv, rs_send, rs_recv, ag_send, ag_recv, side_send, side_recv, fin_send, fin_recv,
    ) = refs[20:]
    slots, rim, edge_slots, own, fan = local.shape[0], lists.shape[2], source.shape[1], coarse_source.shape[1], coarse_source.shape[0]
    halo_rows, row_nodes = 4 * rim, own * n_grp
    blocks = edge_slots // BLOCK
    d, g = lax.axis_index("dom"), lax.axis_index("grp")
    y, x = g // nx, g % nx
    offsets = ring_offsets(ny, nx)
    n = len(offsets)
    ahead = [((y + a) % ny) * nx + (x + b) % nx for a, b in offsets]
    behind = [((y + ny - a) % ny) * nx + (x + nx - b) % nx for a, b in offsets]
    sides = [(d < n_dom - 1, (d + 1, g)), (d > 0, (d - 1, g)), (g < n_grp - 1, (d, g + 1)), (g > 0, (d, g - 1))]
    origins = [d > 0, d < n_dom - 1, g > 0, g < n_grp - 1]

    def remote(src, dst, send, recv, to):
        return pltpu.make_async_remote_copy(src_ref=src, dst_ref=dst, send_sem=send, recv_sem=recv, device_id=to, device_id_type=MESH)

    def all_of(ref, sem):
        pltpu.make_async_copy(ref, ref, sem).wait()

    barrier = pltpu.get_barrier_semaphore()
    for k in ahead:
        pl.semaphore_signal(barrier, inc=1, device_id=(d, k), device_id_type=MESH)
    for there, to in sides[:2]:
        @pl.when(there)
        def _():
            pl.semaphore_signal(barrier, inc=1, device_id=to, device_id_type=MESH)

    places = {
        "send_lists": lists, "node_latent": local.at[:, :L], "node_tangent": local.at[:, L:], "edge_first": edge_first,
        "edge_source": source, "edge_target": target, "edge_latent": edges, "edge_second": edge_second,
        "node_first": node_first, "node_second": node_second, "coarse_owner": owner,
        "coarse_source": coarse_source, "message_first": message_first, "message_second": message_second,
        "coarse_first": coarse_first, "coarse_second": coarse_second, "prolong_first": prolong_first, "prolong_second": prolong_second,
    }
    groups = (
        ("send_lists", "node_latent", "node_tangent", "edge_first"),
        ("edge_source", "edge_target", "edge_latent", "edge_second"),
        NAMES[6:8] + NAMES[10:],
    )
    loads = [[pltpu.make_async_copy(hbm[name], places[name], load_sem.at[i]) for name in group] for i, group in enumerate(groups)]
    for group in loads:
        for copy in group:
            copy.start()

    def need(i):
        for copy in loads[i]:
            copy.wait()

    mean = weights.at[3]
    weights[3] = twice(jnp.full((L, L), 1.0 / L, F32))
    need(0)
    sent = jnp.concatenate([column(lists[0, b : b + 1, :]) for b in range(4)], 0)
    halo_out[...] = dot(picks(sent, slots), local[...]).astype(BF16).reshape(halo_out.shape)
    weights[0] = twice(edge_first[L : 2 * L, :])
    weights[1] = twice(edge_first[2 * L : 3 * L, :])
    table[:slots, :] = dot(local[...], weights[0]).astype(BF16)
    table[slots : 2 * slots, :] = dot(local[...], weights[1]).astype(BF16)
    need(1)
    weights[2] = twice(centred(edge_second[...]))

    def index_columns(ref, at):
        parts = [column(ref[0:1, pl.ds(pl.multiple_of(at + q * LANES, LANES), LANES)]) for q in range(BLOCK // LANES)]
        return jnp.concatenate(parts, 0)

    def gathered(at, with_halo):
        s, t = index_columns(source, at), index_columns(target, at)
        if not with_halo:
            columns[pl.ds(at, BLOCK), :] = s
        hot = [picks(s, slots), picks(t, slots)] + ([picks(s, halo_rows, slots)] if with_halo else [])
        rows = dot(jnp.concatenate(hot, 1), table[: 2 * slots + (halo_rows if with_halo else 0), :])
        return jnp.concatenate([rows[:, :L] + dot(edges[pl.ds(at, BLOCK), :], edge_first[:L, :]), rows[:, L:]], 1)

    def edge_pair(at, with_halo):
        value = pre[pl.ds(at, BLOCK), :]
        if with_halo:
            value = value + dot(picks(columns[pl.ds(at, BLOCK), :], halo_rows, slots), table[2 * slots :, :])
        up, up_tan = norm_pair(dot(swish_pair(value), weights[2]), mean[...])
        return jnp.concatenate([residual(edges[pl.ds(at, BLOCK), :], up), up_tan.astype(BF16)], 1)

    halo_copies = [remote(halo_out.at[b], halo_in.at[b], halo_send.at[b], halo_recv.at[b], to) for b, (_, to) in enumerate(sides)]

    def ahead_of_halo(i, _):
        at = pl.multiple_of(i * BLOCK, BLOCK)
        pre[pl.ds(at, BLOCK), :] = gathered(at, False)
        return 0

    early = blocks // 2
    for b in range(4):
        @pl.when(jnp.logical_not(origins[b]))
        def _():
            halo_in[b] = jnp.zeros(halo_in.shape[1:], BF16)

    pl.semaphore_wait(barrier, n + jnp.where(d > 0, 1, 0) + jnp.where(d < n_dom - 1, 1, 0))
    for b, (there, _) in enumerate(sides):
        @pl.when(there)
        def _():
            halo_copies[b].start()
    lax.fori_loop(0, early, ahead_of_halo, 0)
    for b, there in enumerate(origins):
        @pl.when(there)
        def _():
            halo_copies[b].wait_recv()
    table[2 * slots :, :] = dot(halo_in[...].reshape(halo_rows, 2 * L), weights[0]).astype(BF16)

    def both_stages(i, _):
        at = pl.multiple_of(i * BLOCK, BLOCK)
        before = pl.multiple_of(at - early * BLOCK, BLOCK)
        rows = gathered(at, True)
        pairs[pl.ds(before, BLOCK), :] = edge_pair(before, True)
        pre[pl.ds(at, BLOCK), :] = rows
        return 0

    def last_stage(i, _):
        at = pl.multiple_of(i * BLOCK, BLOCK)
        pairs[pl.ds(at, BLOCK), :] = edge_pair(at, False)
        return 0

    lax.fori_loop(early, blocks, both_stages, 0)
    lax.fori_loop(early, blocks, last_stage, 0)

    need(2)
    weights[0] = twice(node_first[:L, :])
    weights[1] = twice(node_first[L:, :])
    weights[2] = twice(centred(node_second[...]))
    live = jnp.where(lax.broadcasted_iota(I32, (1, edge_slots), 1) < edge_count, target[...], -1)
    first = local
    half = slots // 2

    def summed(h, _):
        at = pl.multiple_of(h * half, half)
        agg[pl.ds(at, half), :] = dot(picks_down(live - at, half), pairs[...]).astype(BF16)
        return 0

    lax.fori_loop(0, 2, summed, 0)
    hidden = swish_pair(dot(local[...], weights[0]) + dot(agg[...], weights[1]))
    up, up_tan = norm_pair(dot(hidden, weights[2]), mean[...])
    first[...] = jnp.concatenate([residual(local[:, :L], up), residual(local[:, L:], up_tan)], 1)
    live = jnp.where(lax.broadcasted_iota(I32, (1, slots), 1) < node_count, owner[...], -1)
    part[...] = dot(picks_down(live, row_nodes), first[...]).astype(BF16).reshape(part.shape)

    rs = [remote(part.at[ahead[m]], arrived.at[m], rs_send, rs_recv, (d, ahead[m])) for m in range(n)]
    for m in reversed(range(n)):
        rs[m].start()
    weights[0] = twice(message_first[:L, :])
    weights[1] = twice(message_first[L:, :])
    weights[2] = twice(message_second[...])
    weights[4] = twice(coarse_first[:L, :])
    weights[5] = twice(coarse_first[L:, :])
    weights[6] = twice(centred(coarse_second[...]))
    weights[7] = twice(prolong_first[:L, :])
    weights[8] = twice(prolong_first[L:, :])
    weights[9] = twice(centred(prolong_second[...]))
    turned[...] = jnp.zeros_like(turned)
    turned[:fan, :own] = coarse_source[...]
    senders_at = jnp.transpose(turned[...])
    for j in range(fan):
        at = jnp.broadcast_to(senders_at[:own, j : j + 1], (own, LANES)).astype(I16)
        picked_senders[j * own : (j + 1) * own, :] = picks(at, 3 * row_nodes)
    for beyond, slot in ((d == 0, 0), (d == n_dom - 1, 2)):
        @pl.when(beyond)
        def _():
            rows3[slot] = jnp.zeros(rows3.shape[1:], BF16)

    mine = part[g].astype(F32)
    all_of(arrived, rs_recv)
    for m in range(n):
        mine = mine + arrived[m].astype(F32)
    mine = mine.astype(BF16)
    rows3[1, g] = mine

    ag = [remote(rows3.at[1, g], rows3.at[1, g], ag_send, ag_recv.at[m], (d, ahead[m])) for m in range(n)]
    for m in reversed(range(n)):
        ag[m].start()

    def passed_on(k):
        up = remote(rows3.at[1, k], rows3.at[0, k], side_send.at[0], side_recv.at[0], (d + 1, g))
        down = remote(rows3.at[1, k], rows3.at[2, k], side_send.at[1], side_recv.at[1], (d - 1, g))
        return up, down

    forwards = [passed_on(behind[m]) for m in range(n)] + [passed_on(g)]

    def forward(m):
        up, down = forwards[m]
        @pl.when(d < n_dom - 1)
        def _():
            up.start()
        @pl.when(d > 0)
        def _():
            down.start()

    forward(n)
    for q in range(slots // LANES):
        picked[q * LANES : (q + 1) * LANES, :] = picks(column(owner[0:1, q * LANES : (q + 1) * LANES]), row_nodes)
    base[...] = dot(first[...], weights[7])
    for m in range(n):
        remote(rows3.at[1, behind[m]], rows3.at[1, behind[m]], ag_send, ag_recv.at[m], (d, ahead[m])).wait_recv()
        forward(m)
    senders = dot(picked_senders[:, row_nodes : 2 * row_nodes], rows3[1].reshape(row_nodes, 2 * L))
    receiver = dot(mine, weights[1])
    @pl.when(d > 0)
    def _():
        all_of(rows3.at[0], side_recv.at[0])
    @pl.when(d < n_dom - 1)
    def _():
        all_of(rows3.at[2], side_recv.at[1])
    senders = senders + dot(picked_senders[:, :row_nodes], rows3[0].reshape(row_nodes, 2 * L))
    senders = senders + dot(picked_senders[:, 2 * row_nodes :], rows3[2].reshape(row_nodes, 2 * L))
    hidden = swish_pair(dot(senders.astype(BF16), weights[0]) + jnp.concatenate([receiver] * fan, 0))
    terms = dot(hidden, weights[2])
    message = terms[:own]
    for j in range(1, fan):
        message = message + terms[j * own : (j + 1) * own]
    hidden = swish_pair(dot(mine, weights[4]) + dot(message.astype(BF16), weights[5]))
    up, up_tan = norm_pair(dot(hidden, weights[6]), mean[...])
    updated[g] = jnp.concatenate([up.astype(BF16), up_tan.astype(BF16)], 1)
    fin = [remote(updated.at[g], updated.at[g], fin_send, fin_recv, (d, ahead[m])) for m in range(n)]
    for m in reversed(range(n)):
        fin[m].start()

    for b, (there, _) in enumerate(sides):
        @pl.when(there)
        def _():
            halo_copies[b].wait_send()
    all_of(arrived, rs_send)
    all_of(arrived, ag_send)
    @pl.when(d < n_dom - 1)
    def _():
        all_of(rows3.at[0], side_send.at[0])
    @pl.when(d > 0)
    def _():
        all_of(rows3.at[2], side_send.at[1])
    all_of(arrived, fin_recv)
    brought = dot(picked[...], updated[...].reshape(row_nodes, 2 * L)).astype(BF16)
    hidden = swish_pair(base[...] + dot(brought, weights[8]))
    up, up_tan = norm_pair(dot(hidden, weights[9]), mean[...])
    valid = lax.broadcasted_iota(I32, (slots, L), 0) < node_count
    node_output[...] = jnp.where(valid, first[:, :L].astype(F32) + up, 0.0).astype(BF16)
    tangent_output[...] = jnp.where(valid, first[:, L:].astype(F32) + up_tan, 0.0).astype(BF16)
    all_of(arrived, fin_send)


def per_device(sizes, *args):
    n_dom, n_grp, ny, nx = sizes
    named = dict(zip(NAMES[:3] + ("node_counts", "edge_counts") + NAMES[3:], args))
    named["coarse_source"] = named["coarse_source"].T
    counts = [named.pop(name) for name in ("node_counts", "edge_counts")]
    shape = {name: a.shape for name, a in named.items()}
    slots, edge_slots, rim = shape["node_latent"][0], shape["edge_latent"][0], shape["send_lists"][2]
    fan, own = shape["coarse_source"]
    row_nodes = n_grp * own
    others = n_grp - 1
    dma = pltpu.SemaphoreType.DMA
    vmem = pltpu.VMEM
    out = jax.ShapeDtypeStruct((slots, L), BF16)
    return pl.pallas_call(
        functools.partial(layer_kernel, sizes),
        out_shape=(out, out),
        in_specs=[pl.BlockSpec(memory_space=pltpu.SMEM)] * 2 + [pl.BlockSpec(memory_space=pltpu.HBM)] * 18,
        out_specs=(pl.BlockSpec(memory_space=vmem),) * 2,
        scratch_shapes=[vmem((slots, 2 * L), BF16), vmem((edge_slots, L), BF16)]
        + [vmem(shape[name], I32) for name in NAMES[3:8]]
        + [vmem(shape[name], BF16) for name in NAMES[8:]]
        + [
            vmem((4, rim, 2 * L), BF16),
            vmem((4, rim, 2 * L), BF16),
            vmem((2 * slots + 4 * rim, 2 * L), BF16),
            vmem((edge_slots // 2, LANES), I16),
            vmem((edge_slots, 2 * L), F32),
            vmem((edge_slots, 2 * L), BF16),
            vmem((slots, row_nodes), BF16),
            vmem((fan * own, 3 * row_nodes), BF16),
            vmem((slots, 2 * L), F32),
            vmem((10, 2 * L, 2 * L), BF16),
            vmem((n_grp, own, 2 * L), BF16),
            vmem((others, own, 2 * L), BF16),
            vmem((3, n_grp, own, 2 * L), BF16),
            vmem((n_grp, own, 2 * L), BF16),
            vmem((LANES, LANES), I32),
            vmem((slots, 2 * L), BF16),
            dma((3,)), dma((4,)), dma((4,)), dma(()), dma(()), dma(()), dma((others,)), dma((2,)), dma((2,)), dma(()), dma(()),
        ],
        compiler_params=pltpu.CompilerParams(collective_id=0, has_side_effects=True, vmem_limit_bytes=VMEM_LIMIT << 20),
    )(*counts, *[pltpu.with_memory_space_constraint(a, pltpu.HBM) for a in named.values()])


VMEM_LIMIT = 40


def solution(mesh):
    n_dom, n_grp = mesh.shape["dom"], mesh.shape["grp"]
    nx = 4 if n_grp % 4 == 0 and n_grp > 4 else 2
    both = ("dom", "grp")
    rows = P(both, None)
    in_specs = (rows, rows, rows, P(both), P(both), P(both, None, None), rows, rows, rows, rows) + (P(),) * 10
    return jax.shard_map(
        functools.partial(per_device, (n_dom, n_grp, n_grp // nx, nx)),
        mesh=mesh, in_specs=in_specs, out_specs=(rows, rows), check_vma=False,
    )
```

time: 57.4 us -> 48.1 us (0.84)
  Pallas kernels: 53.5 us -> 44.6 us
    pallas_call x2 -> x1, Pallas kernels: 53.5 us -> 44.6 us  [per_device(): pl.pallas_call(functools.partial(layer_kernel, sizes), out_shape=(out, ou...]
    unnamed x1 -> x2, local copies, waits for them, and re-layouts: 1.37 us -> 1.41 us
where the time goes in v2:
time: 48.1 us; the launch traced here: 47.9 us
  Pallas kernels  44.6 us (93%)
  between operations  1.94 us (4%)
  local copies, waits for them, and re-layouts  1.41 us (3%)
    pallas_call x1, Pallas kernels, per_device(): pl.pallas_call(functools.partial(layer_kernel, sizes), out_shape=(out, ou...  44.6 us
    unnamed x2, local copies, waits for them, and re-layouts  1.41 us

profile of v2, /device:TPU:1, one launch (start us, length us, event | category | flops | bytes accessed | tf_op | source)
XLA Modules:
  0.0 47.9 jit_solution(2019954945902264846)
XLA Ops:
  1.9 44.6 %shard_map.203 = (bf16[1024,128]{1,0:T(8,128)(2,1)S(1)}, bf16[1024,128]{1,0:T(8,128)(2,1)S(1)}) custom-call(s32[1]{0:T(128)S(6)} %copy.24.refs_0_, s32[1]{0:T(128)S(6)} %copy.25.refs_1_, bf16[1024,128]{1,0:T(8,128)(2,1)} %refs_2_.1, bf16[1024,128]{1,0:T(8,128)(2,1)} %refs_3_.1, bf16[4096,128]{1,0:T(8,128)(2,1)} %refs_4_.1, s32[1,4,128]{2,1,0:T(4,128)} %refs_5_.1, ...), custom_call_target="tpu_custom_call" | custom-call | tf_op jit(solution)/shard_map/pallas_call | solution.py:349
  46.5 0.7 %copy.26 = bf16[1024,128]{1,0:T(8,128)(2,1)} copy(bf16[1024,128]{1,0:T(8,128)(2,1)S(1)} %get-tuple-element.4) | data formatting | bytes 524288
  47.2 0.7 %copy.27 = bf16[1024,128]{1,0:T(8,128)(2,1)} copy(bf16[1024,128]{1,0:T(8,128)(2,1)S(1)} %get-tuple-element.5) | data formatting | bytes 524288

commit v3 on v2

--- a/solution.py
+++ b/solution.py
@@ -51,6 +51,13 @@
     return y, r * ct - y * (r * r * stats[:, L:])
 
 
+def norm_pair_lanes(value):
+    c, ct = value[:, :L], value[:, L:]
+    r = lax.rsqrt(jnp.mean(c * c, axis=-1, keepdims=True) + 1e-5)
+    y = c * r
+    return y, r * ct - y * (r * r * jnp.mean(c * ct, axis=-1, keepdims=True))
+
+
 def column(row):
     return jnp.transpose(jnp.broadcast_to(row, (LANES, LANES))).astype(I16)
 
@@ -90,7 +97,7 @@
         node_output, tangent_output,
         local, edges, lists, source, target, owner, coarse_source,
         edge_first, edge_second, node_first, node_second, message_first, message_second, coarse_first, coarse_second, prolong_first, prolong_second,
-        halo_out, halo_in, table, columns, pre, pairs, picked, picked_senders, base, weights, part, arrived, rows3, updated, turned, agg,
+        halo_out, halo_in, table, columns, pre, pairs, picked, picked_senders, base, weights, part, arrived, rows3, updated, turned, agg, owners_down, sent,
         load_sem, halo_send, halo_recv, rs_send, rs_recv, ag_send, ag_recv, side_send, side_recv, fin_send, fin_recv,
     ) = refs[20:]
     slots, rim, edge_slots, own, fan = local.shape[0], lists.shape[2], source.shape[1], coarse_source.shape[1], coarse_source.shape[0]
@@ -127,24 +134,33 @@
         "coarse_first": coarse_first, "coarse_second": coarse_second, "prolong_first": prolong_first, "prolong_second": prolong_second,
     }
     groups = (
-        ("send_lists", "node_latent", "node_tangent", "edge_first"),
+        ("node_latent", "node_tangent", "edge_first"),
         ("edge_source", "edge_target", "edge_latent", "edge_second"),
         NAMES[6:8] + NAMES[10:],
+        ("send_lists",),
     )
     loads = [[pltpu.make_async_copy(hbm[name], places[name], load_sem.at[i]) for name in group] for i, group in enumerate(groups)]
-    for group in loads:
-        for copy in group:
+
+    def bring(i):
+        for copy in loads[i]:
             copy.start()
 
     def need(i):
         for copy in loads[i]:
             copy.wait()
 
+    bring(3)
+    bring(0)
+
     mean = weights.at[3]
     weights[3] = twice(jnp.full((L, L), 1.0 / L, F32))
+    need(3)
+    for b in range(4):
+        sent[b * rim : (b + 1) * rim, :] = picks(column(lists[0, b : b + 1, :]), slots)
     need(0)
-    sent = jnp.concatenate([column(lists[0, b : b + 1, :]) for b in range(4)], 0)
-    halo_out[...] = dot(picks(sent, slots), local[...]).astype(BF16).reshape(halo_out.shape)
+    bring(1)
+    bring(2)
+    halo_out[...] = dot(sent[...], local[...]).astype(BF16).reshape(halo_out.shape)
     weights[0] = twice(edge_first[L : 2 * L, :])
     weights[1] = twice(edge_first[2 * L : 3 * L, :])
     table[:slots, :] = dot(local[...], weights[0]).astype(BF16)
@@ -168,7 +184,8 @@
         value = pre[pl.ds(at, BLOCK), :]
         if with_halo:
             value = value + dot(picks(columns[pl.ds(at, BLOCK), :], halo_rows, slots), table[2 * slots :, :])
-        up, up_tan = norm_pair(dot(swish_pair(value), weights[2]), mean[...])
+        value = dot(swish_pair(value), weights[2])
+        up, up_tan = norm_pair_lanes(value) if with_halo else norm_pair(value, mean[...])
         return jnp.concatenate([residual(edges[pl.ds(at, BLOCK), :], up), up_tan.astype(BF16)], 1)
 
     halo_copies = [remote(halo_out.at[b], halo_in.at[b], halo_send.at[b], halo_recv.at[b], to) for b, (_, to) in enumerate(sides)]
@@ -200,6 +217,9 @@
         at = pl.multiple_of(i * BLOCK, BLOCK)
         before = pl.multiple_of(at - early * BLOCK, BLOCK)
         rows = gathered(at, True)
+        share = row_nodes // early
+        to = pl.multiple_of((i - early) * share, share)
+        owners_down[pl.ds(to, share), :] = picks_down(kept - to, share)
         pairs[pl.ds(before, BLOCK), :] = edge_pair(before, True)
         pre[pl.ds(at, BLOCK), :] = rows
         return 0
@@ -207,13 +227,19 @@
     def last_stage(i, _):
         at = pl.multiple_of(i * BLOCK, BLOCK)
         pairs[pl.ds(at, BLOCK), :] = edge_pair(at, False)
+        rows = pl.ds(pl.multiple_of((i - early) * (slots // early), slots // early), slots // early)
+        base[rows, :] = dot(local[rows, :], weights[10])
         return 0
 
+    need(2)
+    node = owner[...]
+    piece = own // 2
+    node = lax.rem(lax.div(node, piece), 2) * (row_nodes // 2) + lax.div(node, own) * piece + lax.rem(node, piece)
+    kept = jnp.where(lax.broadcasted_iota(I32, (1, slots), 1) < node_count, node, -1)
+    weights[10] = twice(node_first[:L, :])
     lax.fori_loop(early, blocks, both_stages, 0)
     lax.fori_loop(early, blocks, last_stage, 0)
 
-    need(2)
-    weights[0] = twice(node_first[:L, :])
     weights[1] = twice(node_first[L:, :])
     weights[2] = twice(centred(node_second[...]))
     live = jnp.where(lax.broadcasted_iota(I32, (1, edge_slots), 1) < edge_count, target[...], -1)
@@ -226,20 +252,18 @@
         return 0
 
     lax.fori_loop(0, 2, summed, 0)
-    hidden = swish_pair(dot(local[...], weights[0]) + dot(agg[...], weights[1]))
+    hidden = swish_pair(base[...] + dot(agg[...], weights[1]))
     up, up_tan = norm_pair(dot(hidden, weights[2]), mean[...])
     first[...] = jnp.concatenate([residual(local[:, :L], up), residual(local[:, L:], up_tan)], 1)
-    live = jnp.where(lax.broadcasted_iota(I32, (1, slots), 1) < node_count, owner[...], -1)
-    part[...] = dot(picks_down(live, row_nodes), first[...]).astype(BF16).reshape(part.shape)
-
-    rs = [remote(part.at[ahead[m]], arrived.at[m], rs_send, rs_recv, (d, ahead[m])) for m in range(n)]
-    for m in reversed(range(n)):
-        rs[m].start()
+    for c in range(2):
+        some = slice(c * (row_nodes // 2), (c + 1) * (row_nodes // 2))
+        part[c] = dot(owners_down[some, :], first[...]).astype(BF16).reshape(part.shape[1:])
+        for m in reversed(range(n)):
+            remote(part.at[c, ahead[m]], arrived.at[c, m], rs_send, rs_recv.at[c], (d, ahead[m])).start()
     weights[0] = twice(message_first[:L, :])
     weights[1] = twice(message_first[L:, :])
-    weights[2] = twice(message_second[...])
     weights[4] = twice(coarse_first[:L, :])
-    weights[5] = twice(coarse_first[L:, :])
+    weights[5] = twice(dot(message_second[...], coarse_first[L:, :]))
     weights[6] = twice(centred(coarse_second[...]))
     weights[7] = twice(prolong_first[:L, :])
     weights[8] = twice(prolong_first[L:, :])
@@ -255,16 +279,16 @@
         def _():
             rows3[slot] = jnp.zeros(rows3.shape[1:], BF16)
 
-    mine = part[g].astype(F32)
-    all_of(arrived, rs_recv)
-    for m in range(n):
-        mine = mine + arrived[m].astype(F32)
-    mine = mine.astype(BF16)
-    rows3[1, g] = mine
-
-    ag = [remote(rows3.at[1, g], rows3.at[1, g], ag_send, ag_recv.at[m], (d, ahead[m])) for m in range(n)]
-    for m in reversed(range(n)):
-        ag[m].start()
+    for c in range(2):
+        rows = pl.ds(c * piece, piece)
+        all_of(arrived.at[c], rs_recv.at[c])
+        total = part[c, g].astype(F32)
+        for m in range(n):
+            total = total + arrived[c, m].astype(F32)
+        rows3[1, g, rows] = total.astype(BF16)
+        for m in reversed(range(n)):
+            remote(rows3.at[1, g, rows], rows3.at[1, g, rows], ag_send, ag_recv.at[m], (d, ahead[m])).start()
+    mine = rows3[1, g]
 
     def passed_on(k):
         up = remote(rows3.at[1, k], rows3.at[0, k], side_send.at[0], side_recv.at[0], (d + 1, g))
@@ -291,6 +315,7 @@
         forward(m)
     senders = dot(picked_senders[:, row_nodes : 2 * row_nodes], rows3[1].reshape(row_nodes, 2 * L))
     receiver = dot(mine, weights[1])
+    own_part = dot(mine, weights[4])
     @pl.when(d > 0)
     def _():
         all_of(rows3.at[0], side_recv.at[0])
@@ -300,12 +325,11 @@
     senders = senders + dot(picked_senders[:, :row_nodes], rows3[0].reshape(row_nodes, 2 * L))
     senders = senders + dot(picked_senders[:, 2 * row_nodes :], rows3[2].reshape(row_nodes, 2 * L))
     hidden = swish_pair(dot(senders.astype(BF16), weights[0]) + jnp.concatenate([receiver] * fan, 0))
-    terms = dot(hidden, weights[2])
-    message = terms[:own]
+    message = hidden[:own].astype(F32)
     for j in range(1, fan):
-        message = message + terms[j * own : (j + 1) * own]
-    hidden = swish_pair(dot(mine, weights[4]) + dot(message.astype(BF16), weights[5]))
-    up, up_tan = norm_pair(dot(hidden, weights[6]), mean[...])
+        message = message + hidden[j * own : (j + 1) * own].astype(F32)
+    hidden = swish_pair(own_part + dot(message.astype(BF16), weights[5]))
+    up, up_tan = norm_pair_lanes(dot(hidden, weights[6]))
     updated[g] = jnp.concatenate([up.astype(BF16), up_tan.astype(BF16)], 1)
     fin = [remote(updated.at[g], updated.at[g], fin_send, fin_recv, (d, ahead[m])) for m in range(n)]
     for m in reversed(range(n)):
@@ -324,13 +348,21 @@
     def _():
         all_of(rows3.at[2], side_send.at[1])
     all_of(arrived, fin_recv)
-    brought = dot(picked[...], updated[...].reshape(row_nodes, 2 * L)).astype(BF16)
-    hidden = swish_pair(base[...] + dot(brought, weights[8]))
+    brought = dot(updated[...].reshape(row_nodes, 2 * L), weights[8]).astype(BF16)
+    hidden = swish_pair(base[...] + dot(picked[...], brought))
     up, up_tan = norm_pair(dot(hidden, weights[9]), mean[...])
     valid = lax.broadcasted_iota(I32, (slots, L), 0) < node_count
     node_output[...] = jnp.where(valid, first[:, :L].astype(F32) + up, 0.0).astype(BF16)
     tangent_output[...] = jnp.where(valid, first[:, L:].astype(F32) + up_tan, 0.0).astype(BF16)
     all_of(arrived, fin_send)
+
+
+def store_kernel(primal, tan, node_output, tangent_output, sems):
+    copies = [pltpu.make_async_copy(primal, node_output, sems.at[0]), pltpu.make_async_copy(tan, tangent_output, sems.at[1])]
+    for copy in copies:
+        copy.start()
+    for copy in copies:
+        copy.wait()
 
 
 def per_device(sizes, *args):
@@ -346,7 +378,7 @@
     dma = pltpu.SemaphoreType.DMA
     vmem = pltpu.VMEM
     out = jax.ShapeDtypeStruct((slots, L), BF16)
-    return pl.pallas_call(
+    results = pl.pallas_call(
         functools.partial(layer_kernel, sizes),
         out_shape=(out, out),
         in_specs=[pl.BlockSpec(memory_space=pltpu.SMEM)] * 2 + [pl.BlockSpec(memory_space=pltpu.HBM)] * 18,
@@ -364,17 +396,26 @@
             vmem((slots, row_nodes), BF16),
             vmem((fan * own, 3 * row_nodes), BF16),
             vmem((slots, 2 * L), F32),
-            vmem((10, 2 * L, 2 * L), BF16),
-            vmem((n_grp, own, 2 * L), BF16),
-            vmem((others, own, 2 * L), BF16),
+            vmem((11, 2 * L, 2 * L), BF16),
+            vmem((2, n_grp, own // 2, 2 * L), BF16),
+            vmem((2, others, own // 2, 2 * L), BF16),
             vmem((3, n_grp, own, 2 * L), BF16),
             vmem((n_grp, own, 2 * L), BF16),
             vmem((LANES, LANES), I32),
             vmem((slots, 2 * L), BF16),
-            dma((3,)), dma((4,)), dma((4,)), dma(()), dma(()), dma(()), dma((others,)), dma((2,)), dma((2,)), dma(()), dma(()),
+            vmem((row_nodes, slots), BF16),
+            vmem((4 * rim, slots), BF16),
+            dma((4,)), dma((4,)), dma((4,)), dma(()), dma((2,)), dma(()), dma((others,)), dma((2,)), dma((2,)), dma(()), dma(()),
         ],
         compiler_params=pltpu.CompilerParams(collective_id=0, has_side_effects=True, vmem_limit_bytes=VMEM_LIMIT << 20),
     )(*counts, *[pltpu.with_memory_space_constraint(a, pltpu.HBM) for a in named.values()])
+    return pl.pallas_call(
+        store_kernel,
+        out_shape=(out, out),
+        in_specs=[pl.BlockSpec(memory_space=pl.ANY)] * 2,
+        out_specs=(pl.BlockSpec(memory_space=pltpu.HBM),) * 2,
+        scratch_shapes=[dma((2,))],
+    )(*[pltpu.with_memory_space_constraint(a, pltpu.VMEM) for a in results])
 
 
 VMEM_LIMIT = 40

time: 48.1 us -> 46 us (0.956)
  local copies, waits for them, and re-layouts: 1.41 us -> 0 us
  Pallas kernels: 44.6 us -> 43.9 us
    pallas_call x1, Pallas kernels: 44.6 us -> 43.1 us  [per_device(): pl.pallas_call(functools.partial(layer_kernel, sizes), out_shape=(out, ou...]
    unnamed x2 -> x0, local copies, waits for them, and re-layouts: 1.41 us -> none
    pallas_call x0 -> x1, Pallas kernels: none -> 0.81 us  [per_device(): pl.pallas_call(store_kernel, out_shape=(out, out), in_specs=[pl.BlockSpec...]
where the time goes in v3:
time: 46 us; the launch traced here: 45.8 us
  Pallas kernels  43.9 us (95%)
  between operations  1.94 us (4%)
    pallas_call x1, Pallas kernels, per_device(): pl.pallas_call(functools.partial(layer_kernel, sizes), out_shape=(out, ou...  43.1 us

profile of v3, /device:TPU:1, one launch (start us, length us, event | category | flops | bytes accessed | tf_op | source)
XLA Modules:
  0.0 45.8 jit_solution(15439538033708478124)
XLA Ops:
  1.9 43.1 %shard_map.203 = (bf16[1024,128]{1,0:T(8,128)(2,1)S(1)}, bf16[1024,128]{1,0:T(8,128)(2,1)S(1)}) custom-call(s32[1]{0:T(128)S(6)} %copy.22.refs_0_, s32[1]{0:T(128)S(6)} %copy.23.refs_1_, bf16[1024,128]{1,0:T(8,128)(2,1)} %refs_2_.1, bf16[1024,128]{1,0:T(8,128)(2,1)} %refs_3_.1, bf16[4096,128]{1,0:T(8,128)(2,1)} %refs_4_.1, s32[1,4,128]{2,1,0:T(4,128)} %refs_5_.1, ...), custom_call_target="tpu_custom_call" | custom-call | tf_op jit(solution)/shard_map/pallas_call | solution.py:381
  45.0 0.8 %shard_map.204 = (bf16[1024,128]{1,0:T(8,128)(2,1)}, bf16[1024,128]{1,0:T(8,128)(2,1)}) custom-call(bf16[1024,128]{1,0:T(8,128)(2,1)S(1)} %get-tuple-element.4.primal, bf16[1024,128]{1,0:T(8,128)(2,1)S(1)} %get-tuple-element.5.tan), custom_call_target="tpu_custom_call" | custom-call | tf_op jit(solution)/shard_map/pallas_call | solution.py:412

commit v4 on v3

--- a/solution.py
+++ b/solution.py
@@ -134,10 +134,10 @@
         "coarse_first": coarse_first, "coarse_second": coarse_second, "prolong_first": prolong_first, "prolong_second": prolong_second,
     }
     groups = (
-        ("node_latent", "node_tangent", "edge_first"),
+        ("node_latent", "node_tangent"),
         ("edge_source", "edge_target", "edge_latent", "edge_second"),
         NAMES[6:8] + NAMES[10:],
-        ("send_lists",),
+        ("send_lists", "edge_first"),
     )
     loads = [[pltpu.make_async_copy(hbm[name], places[name], load_sem.at[i]) for name in group] for i, group in enumerate(groups)]
 
@@ -157,12 +157,12 @@
     need(3)
     for b in range(4):
         sent[b * rim : (b + 1) * rim, :] = picks(column(lists[0, b : b + 1, :]), slots)
+    weights[0] = twice(edge_first[L : 2 * L, :])
+    weights[1] = twice(edge_first[2 * L : 3 * L, :])
     need(0)
     bring(1)
     bring(2)
     halo_out[...] = dot(sent[...], local[...]).astype(BF16).reshape(halo_out.shape)
-    weights[0] = twice(edge_first[L : 2 * L, :])
-    weights[1] = twice(edge_first[2 * L : 3 * L, :])
     table[:slots, :] = dot(local[...], weights[0]).astype(BF16)
     table[slots : 2 * slots, :] = dot(local[...], weights[1]).astype(BF16)
     need(1)
@@ -253,7 +253,7 @@
 
     lax.fori_loop(0, 2, summed, 0)
     hidden = swish_pair(base[...] + dot(agg[...], weights[1]))
-    up, up_tan = norm_pair(dot(hidden, weights[2]), mean[...])
+    up, up_tan = norm_pair_lanes(dot(hidden, weights[2]))
     first[...] = jnp.concatenate([residual(local[:, :L], up), residual(local[:, L:], up_tan)], 1)
     for c in range(2):
         some = slice(c * (row_nodes // 2), (c + 1) * (row_nodes // 2))
@@ -286,7 +286,7 @@
         for m in range(n):
             total = total + arrived[c, m].astype(F32)
         rows3[1, g, rows] = total.astype(BF16)
-        for m in reversed(range(n)):
+        for m in (range(n) if c == 1 else reversed(range(n))):
             remote(rows3.at[1, g, rows], rows3.at[1, g, rows], ag_send, ag_recv.at[m], (d, ahead[m])).start()
     mine = rows3[1, g]
 
@@ -350,7 +350,7 @@
     all_of(arrived, fin_recv)
     brought = dot(updated[...].reshape(row_nodes, 2 * L), weights[8]).astype(BF16)
     hidden = swish_pair(base[...] + dot(picked[...], brought))
-    up, up_tan = norm_pair(dot(hidden, weights[9]), mean[...])
+    up, up_tan = norm_pair_lanes(dot(hidden, weights[9]))
     valid = lax.broadcasted_iota(I32, (slots, L), 0) < node_count
     node_output[...] = jnp.where(valid, first[:, :L].astype(F32) + up, 0.0).astype(BF16)
     tangent_output[...] = jnp.where(valid, first[:, L:].astype(F32) + up_tan, 0.0).astype(BF16)

time: 46 us -> 45.4 us (0.987)
  Pallas kernels: 43.9 us -> 43.3 us
    pallas_call x1, Pallas kernels: 43.1 us -> 42.5 us  [per_device(): pl.pallas_call(functools.partial(layer_kernel, sizes), out_shape=(out, ou...]
where the time goes in v4:
time: 45.4 us; the launch traced here: 45.3 us
  Pallas kernels  43.3 us (95%)
  between operations  1.94 us (4%)
    pallas_call x1, Pallas kernels, per_device(): pl.pallas_call(functools.partial(layer_kernel, sizes), out_shape=(out, ou...  42.5 us

profile of v4, /device:TPU:1, one launch (start us, length us, event | category | flops | bytes accessed | tf_op | source)
XLA Modules:
  0.0 45.3 jit_solution(5854838896620391567)
XLA Ops:
  1.9 42.5 %shard_map.203 = (bf16[1024,128]{1,0:T(8,128)(2,1)S(1)}, bf16[1024,128]{1,0:T(8,128)(2,1)S(1)}) custom-call(s32[1]{0:T(128)S(6)} %copy.22.refs_0_, s32[1]{0:T(128)S(6)} %copy.23.refs_1_, bf16[1024,128]{1,0:T(8,128)(2,1)} %refs_2_.1, bf16[1024,128]{1,0:T(8,128)(2,1)} %refs_3_.1, bf16[4096,128]{1,0:T(8,128)(2,1)} %refs_4_.1, s32[1,4,128]{2,1,0:T(4,128)} %refs_5_.1, ...), custom_call_target="tpu_custom_call" | custom-call | tf_op jit(solution)/shard_map/pallas_call | solution.py:381
  44.5 0.8 %shard_map.204 = (bf16[1024,128]{1,0:T(8,128)(2,1)}, bf16[1024,128]{1,0:T(8,128)(2,1)}) custom-call(bf16[1024,128]{1,0:T(8,128)(2,1)S(1)} %get-tuple-element.4.primal, bf16[1024,128]{1,0:T(8,128)(2,1)S(1)} %get-tuple-element.5.tan), custom_call_target="tpu_custom_call" | custom-call | tf_op jit(solution)/shard_map/pallas_call | solution.py:412

commit v5 on v4

--- a/solution.py
+++ b/solution.py
@@ -107,8 +107,10 @@
     y, x = g // nx, g % nx
     offsets = ring_offsets(ny, nx)
     n = len(offsets)
-    ahead = [((y + a) % ny) * nx + (x + b) % nx for a, b in offsets]
-    behind = [((y + ny - a) % ny) * nx + (x + nx - b) % nx for a, b in offsets]
+    odd = d % 2
+    turns = [(a + odd * ((ny - a) % ny - a), b + odd * ((nx - b) % nx - b)) for a, b in offsets]
+    ahead = [((y + a) % ny) * nx + (x + b) % nx for a, b in turns]
+    behind = [((y + ny - a) % ny) * nx + (x + nx - b) % nx for a, b in turns]
     sides = [(d < n_dom - 1, (d + 1, g)), (d > 0, (d - 1, g)), (g < n_grp - 1, (d, g + 1)), (g > 0, (d, g - 1))]
     origins = [d > 0, d < n_dom - 1, g > 0, g < n_grp - 1]
 

time: 45.4 us -> 45.6 us (level)
  no operation moved by 1% of the time
where the time goes in v5:
time: 45.6 us; the launch traced here: 45.4 us
  Pallas kernels  43.5 us (95%)
  between operations  1.94 us (4%)
    pallas_call x1, Pallas kernels, per_device(): pl.pallas_call(functools.partial(layer_kernel, sizes), out_shape=(out, ou...  42.7 us

profile of v5, /device:TPU:1, one launch (start us, length us, event | category | flops | bytes accessed | tf_op | source)
XLA Modules:
  0.0 45.4 jit_solution(6823680105976176149)
XLA Ops:
  1.9 42.7 %shard_map.203 = (bf16[1024,128]{1,0:T(8,128)(2,1)S(1)}, bf16[1024,128]{1,0:T(8,128)(2,1)S(1)}) custom-call(s32[1]{0:T(128)S(6)} %copy.22.refs_0_, s32[1]{0:T(128)S(6)} %copy.23.refs_1_, bf16[1024,128]{1,0:T(8,128)(2,1)} %refs_2_.1, bf16[1024,128]{1,0:T(8,128)(2,1)} %refs_3_.1, bf16[4096,128]{1,0:T(8,128)(2,1)} %refs_4_.1, s32[1,4,128]{2,1,0:T(4,128)} %refs_5_.1, ...), custom_call_target="tpu_custom_call" | custom-call | tf_op jit(solution)/shard_map/pallas_call | solution.py:383
  44.6 0.8 %shard_map.204 = (bf16[1024,128]{1,0:T(8,128)(2,1)}, bf16[1024,128]{1,0:T(8,128)(2,1)}) custom-call(bf16[1024,128]{1,0:T(8,128)(2,1)S(1)} %get-tuple-element.4.primal, bf16[1024,128]{1,0:T(8,128)(2,1)S(1)} %get-tuple-element.5.tan), custom_call_target="tpu_custom_call" | custom-call | tf_op jit(solution)/shard_map/pallas_call | solution.py:414
